TPU v7x, 256 devices: a whole 4x4x8 slice. The times are simulated.
256 devices in a mesh: chan: 16 (over z, x_lo), stn: 16 (over x_hi, y, core).
Axes of the slice: x: 4 (x_hi: 2, x_lo: 2; x = x_hi * 2 + x_lo), y: 4, z: 8, core: 2. Of those that a mesh axis runs over, the one named last changes fastest.
Arguments:
- voltages: bfloat16 [128, 512, 4096], P('chan', 'stn'), may hold values from -6 to 6
- kernels: bfloat16 [128, 2, 8], P('chan'), may hold values from 0.049804688 to 0.5
- tile_lists: int32 [128, 16, 64, 128], P('chan', 'stn'), may hold values from 0 to 9216, as said below
- offset_u: int32 [128, 16, 64, 128], P('chan', 'stn'), may hold values from 0 to 24
- offset_v: int32 [128, 16, 64, 128], P('chan', 'stn'), may hold values from 0 to 24
- owner_map: int32 [128, 64], P('chan'), may hold values from 0 to 255
Outputs:
- grid_tiles: float32 [256, 2048], P(('chan', 'stn'))
Inputs may be any that keep to these rules, and one draw needn't show every extreme that they name: `tile_lists`: each list holds its live baseline indices first and the value 9 * 32 * 32 (no baseline) in the remaining slots; in every channel and group one tile's list is full, and the others hold 32 to 128 live entries; no baseline appears twice in one channel and group while 64 * 128 <= 9216.
All inputs are finite; a program needn't handle non-finite values.
Results may differ from a plain program's by a relative error of at most 0.004.
Values may be sent and summed in bfloat16 or wider, within the bound.
A program may use at most 128 MiB of HBM per device.

v0:
```python
import math

import jax
import jax.numpy as jnp
from jax import lax
from jax.sharding import PartitionSpec as P

TILE = 32
TILES_DEV = 1


def from_behind(value, axis, steps):
    count = lax.axis_size(axis)
    pairs = [(source, (source + steps) % count) for source in range(count)]
    return lax.ppermute(value, axis, pairs)


def rotate_parts(block):
    half_width = block.shape[-1] // 2
    return jnp.concatenate([-block[..., half_width:], block[..., :half_width]], axis=-1)


def kernel_rows(offsets, taps):
    cell_ids = jnp.arange(TILE, dtype=jnp.int32)
    distance = cell_ids[None, None, None, :] - offsets[..., None]
    result = jnp.zeros(distance.shape, jnp.float32)
    for tap in range(taps.shape[-1]):
        result = result + jnp.where(
            distance == tap, taps[:, tap].astype(jnp.float32)[:, None, None, None], jnp.float32(0.0)
        )
    return result


def pick_channel(inputs):
    table, entry_ids = inputs
    n_rows, row_width = table.shape
    n_group = row_width // 2
    high_part = entry_ids // n_group
    low_part = entry_ids - high_part * n_group
    row_hot = (high_part[:, None] == jnp.arange(n_rows, dtype=jnp.int32)[None, :]).astype(
        jnp.bfloat16
    )
    chosen_rows = jnp.dot(row_hot, table, preferred_element_type=jnp.float32)
    col_hot = (low_part[:, None] == jnp.arange(n_group, dtype=jnp.int32)[None, :]).astype(
        jnp.float32
    )
    values = jnp.sum(
        chosen_rows.reshape(entry_ids.shape[0], 2, n_group) * col_hot[:, None, :], axis=-1
    )
    return values.astype(jnp.bfloat16)


def on_device(voltages, kernels, tile_lists, offset_u, offset_v, owner_map):
    n_chan, n_group, width = voltages.shape
    n_tiles, capacity = (tile_lists.shape[2], tile_lists.shape[3])
    n_loop = lax.axis_size("stn")
    half_loop = n_loop // 2
    shifts = half_loop + 1
    my_index = lax.axis_index("stn")
    norm_scale = 1.0 / math.sqrt(width)

    def correlate(other):
        paired = jnp.concatenate([other, rotate_parts(other)], axis=1)
        return (
            jnp.einsum("cik,cjk->cij", voltages, paired, preferred_element_type=jnp.float32)
            * norm_scale
        )

    blocks = [None] * shifts
    blocks[0] = correlate(voltages)
    moving = voltages
    for step_count in range(1, half_loop + 1):
        moving = from_behind(moving, "stn", -1)
        blocks[step_count] = correlate(moving)
    stacked = jnp.stack(blocks, axis=1).reshape(n_chan, shifts, n_group, 2, n_group)
    shift_ids = jnp.arange(shifts, dtype=jnp.int32)[None, :, None, None, None]
    row_ids = jnp.arange(n_group, dtype=jnp.int32)[None, None, :, None, None]
    col_ids = jnp.arange(n_group, dtype=jnp.int32)[None, None, None, None, :]
    auto_mask = (shift_ids == 0) & (row_ids == col_ids)
    far_mask = (shift_ids == half_loop) & (my_index >= half_loop)
    kept_mask = jnp.logical_not(auto_mask | far_mask)
    vis = jnp.where(kept_mask, stacked, jnp.float32(0.0)).astype(jnp.bfloat16)
    vis_table = vis.reshape(n_chan, shifts * n_group, 2 * n_group)
    entry_ids = tile_lists.reshape(n_chan, n_tiles * capacity)
    picked = lax.map(pick_channel, (vis_table, entry_ids))
    picked = picked.reshape(n_chan, n_tiles, capacity, 2)
    row_taps = kernel_rows(offset_u.reshape(n_chan, n_tiles, capacity), kernels[:, 0, :]).astype(
        jnp.bfloat16
    )
    col_taps = kernel_rows(offset_v.reshape(n_chan, n_tiles, capacity), kernels[:, 1, :])
    weighted = (picked.astype(jnp.float32)[..., :, None] * col_taps[..., None, :]).astype(
        jnp.bfloat16
    )
    tile_grid = jnp.einsum(
        "ctku,ctkrv->ctruv", row_taps, weighted, preferred_element_type=jnp.float32
    )
    grid_rows = tile_grid.reshape(n_chan * n_tiles, -1)
    n_global = TILES_DEV * lax.axis_size("chan") * lax.axis_size("stn")
    owner_hot = (
        jnp.arange(n_global, dtype=jnp.int32)[:, None] == owner_map.reshape(-1)[None, :]
    ).astype(jnp.float32)
    partial_grid = jnp.dot(
        owner_hot, grid_rows, precision=lax.Precision.HIGHEST, preferred_element_type=jnp.float32
    )
    return lax.psum_scatter(partial_grid, ("chan", "stn"), scatter_dimension=0, tiled=True)


def solution(mesh):
    placed = (
        P("chan", "stn", None),
        P("chan", None, None),
        P("chan", "stn", None, None),
        P("chan", "stn", None, None),
        P("chan", "stn", None, None),
        P("chan", None),
    )
    return jax.shard_map(
        on_device, mesh=mesh, in_specs=placed, out_specs=P(("chan", "stn"), None), check_vma=False
    )
```

profile of v0, /device:TPU:2, one launch (start us, length us, event | category | flops | bytes accessed | tf_op | source)
XLA Modules:
  0.0 579.3 jit_solution(5271098234347581570)
XLA Ops:
  6.5 4.0 collective-permute-start
  10.6 23.9 %collective-permute-done = bf16[8,32,4096]{2,1,0:T(8,128)(2,1)S(1)} collective-permute-done((bf16[8,32,4096]{2,1,0:T(8,128)(2,1)}, bf16[8,32,4096]{2,1,0:T(8,128)(2,1)S(1)}, u32[]{:S(2)}, u32[]{:S(2)}) %collective-permute-start) | collective-permute-done | bytes 2097184 | tf_op jit(solution)/shard_map/ppermute | solution.py:15
  34.4 5.4 collective-permute-start.1
  39.8 23.6 %collective-permute-done.1 = bf16[8,32,4096]{2,1,0:T(8,128)(2,1)S(1)} collective-permute-done((bf16[8,32,4096]{2,1,0:T(8,128)(2,1)S(1)}, bf16[8,32,4096]{2,1,0:T(8,128)(2,1)S(1)}, u32[]{:S(2)}, u32[]{:S(2)}) %collective-permute-start.1) | collective-permute-done | bytes 2097184 | tf_op jit(solution)/shard_map/ppermute | solution.py:15
  63.4 5.5 collective-permute-start.2
  69.9 22.5 %collective-permute-done.2 = bf16[8,32,4096]{2,1,0:T(8,128)(2,1)S(1)} collective-permute-done((bf16[8,32,4096]{2,1,0:T(8,128)(2,1)S(1)}, bf16[8,32,4096]{2,1,0:T(8,128)(2,1)S(1)}, u32[]{:S(2)}, u32[]{:S(2)}) %collective-permute-start.2) | collective-permute-done | bytes 2097184 | tf_op jit(solution)/shard_map/ppermute | solution.py:15
  92.5 5.5 collective-permute-start.3
  99.7 8.1 %select_add_fusion = f32[8,64,128,32]{2,3,1,0:T(8,128)} fusion(f32[8]{0:T(128)S(1)} %get-tuple-element.77, f32[8]{0:T(128)S(1)} %get-tuple-element.78, f32[8]{0:T(128)S(1)} %get-tuple-element.79, f32[8]{0:T(128)S(1)} %get-tuple-element.80, f32[8]{0:T(128)S(1)} %get-tuple-element.81, f32[8]{0:T(128)S(1)} %get-tuple-element.82, f32[8]{0:T(128)S(1)} %get-tuple-element.83, ...), kind=kLoop, calls=%fused_computation.32 | loop fusion | flops 50331648 | bytes 8651008 | tf_op jit(solution)/shard_map/add | solution.py:28
  107.8 13.7 %collective-permute-done.3 = bf16[8,32,4096]{2,1,0:T(8,128)(2,1)} collective-permute-done((bf16[8,32,4096]{2,1,0:T(8,128)(2,1)S(1)}, bf16[8,32,4096]{2,1,0:T(8,128)(2,1)}, u32[]{:S(2)}, u32[]{:S(2)}) %collective-permute-start.3) | collective-permute-done | bytes 2097184 | tf_op jit(solution)/shard_map/ppermute | solution.py:15
  121.6 5.6 collective-permute-start.4
  138.9 12.2 %collective-permute-done.4 = bf16[8,32,4096]{2,1,0:T(8,128)(2,1)} collective-permute-done((bf16[8,32,4096]{2,1,0:T(8,128)(2,1)}, bf16[8,32,4096]{2,1,0:T(8,128)(2,1)}, u32[]{:S(2)}, u32[]{:S(2)}) %collective-permute-start.4) | collective-permute-done | bytes 2097184 | tf_op jit(solution)/shard_map/ppermute | solution.py:15
  151.0 5.5 collective-permute-start.5
  169.3 11.2 %collective-permute-done.5 = bf16[8,32,4096]{2,1,0:T(8,128)(2,1)} collective-permute-done((bf16[8,32,4096]{2,1,0:T(8,128)(2,1)}, bf16[8,32,4096]{2,1,0:T(8,128)(2,1)}, u32[]{:S(2)}, u32[]{:S(2)}) %collective-permute-start.5) | collective-permute-done | bytes 2097184 | tf_op jit(solution)/shard_map/ppermute | solution.py:15
  180.4 5.5 collective-permute-start.6
  187.6 3.5 fusion.132
  201.5 8.4 %collective-permute-done.6 = bf16[8,32,4096]{2,1,0:T(8,128)(2,1)} collective-permute-done((bf16[8,32,4096]{2,1,0:T(8,128)(2,1)}, bf16[8,32,4096]{2,1,0:T(8,128)(2,1)}, u32[]{:S(2)}, u32[]{:S(2)}) %collective-permute-start.6) | collective-permute-done | bytes 2097184 | tf_op jit(solution)/shard_map/ppermute | solution.py:15
  209.8 5.5 collective-permute-start.7
  230.8 8.4 %collective-permute-done.7 = bf16[8,32,4096]{2,1,0:T(8,128)(2,1)} collective-permute-done((bf16[8,32,4096]{2,1,0:T(8,128)(2,1)}, bf16[8,32,4096]{2,1,0:T(8,128)(2,1)}, u32[]{:S(2)}, u32[]{:S(2)}) %collective-permute-start.7) | collective-permute-done | bytes 2097184 | tf_op jit(solution)/shard_map/ppermute | solution.py:15
  247.3 18.0 %while.12 = (s32[]{:T(128)}, bf16[8,8192,2]{1,2,0:T(2,128)(2,1)S(1)}, s32[8,8192]{1,0:T(8,128)S(1)}, bf16[8,288,64]{1,2,0:T(8,128)(2,1)S(1)}, s32[]{:T(128)}) while((s32[]{:T(128)}, bf16[8,8192,2]{1,2,0:T(2,128)(2,1)S(1)}, s32[8,8192]{1,0:T(8,128)S(1)}, bf16[8,288,64]{1,2,0:T(8,128)(2,1)S(1)}, s32[]{:T(128)}) %tuple.63), condition=%wide.region_2.3_spmd, body=%wide.region_0.2_spmd.sunk | while | flops 306044928 | bytes 2535497 | solution.py:85
  265.5 13.2 %convolution_bitcast_fusion = f32[8,64,2,32,32]{3,4,2,1,0:T(8,128)} fusion(f32[8,64,128,32]{2,3,1,0:T(8,128)} %select_add_fusion, f32[8,64,128,2]{2,3,1,0:T(2,128)S(1)} %bitcast_convert_fusion, f32[8]{0:T(128)S(1)} %get-tuple-element.69, f32[8]{0:T(128)S(1)} %get-tuple-element.70, f32[8]{0:T(128)S(1)} %copy-done.11, f32[8]{0:T(128)S(1)} %copy-done.12, ...), kind=kOutput, calls=%fused_computation.20 | convolution fusion | flops 329252864 | bytes 13369600 | tf_op jit(solution)/shard_map/ctku,ctkrv->ctruv/dot_general | solution.py:94
  278.8 13.8 %copy.40 = f32[8,64,2,32,32]{1,0,4,3,2:T(8,128)} copy(f32[8,64,2,32,32]{3,4,2,1,0:T(8,128)} %convolution_bitcast_fusion) | data formatting | bytes 8388608 | tf_op jit(solution)/shard_map/ctku,ctkrv->ctruv/transpose | solution.py:94
  292.6 7.5 %reshape.314 = f32[512,2048]{0,1:T(8,128)} reshape(f32[8,64,2,32,32]{1,0,4,3,2:T(8,128)} %copy.40) | data formatting | bytes 8388608 | tf_op jit(solution)/shard_map/reshape | solution.py:97
  300.1 5.8 %fusion.159 = f32[256,2048]{1,0:T(8,128)} fusion(f32[512,2048]{0,1:T(8,128)} %reshape.314, s32[512]{0:T(512)S(1)} %eq.170), kind=kOutput, calls=%fused_computation.145 | convolution fusion | flops 3221356544 | bytes 6293504 | tf_op jit(solution)/shard_map/dot_general | solution.py:102
  305.9 265.1 %all-reduce.3.cloned.1.call-done = f32[256,2048]{1,0:T(8,128)} async-done(((f32[256,2048]{1,0:T(8,128)}), f32[256,2048]{1,0:T(8,128)}) %all-reduce.3.cloned.1.call-update) | async-done | bytes 2097168
  (137 shorter events, 81.5 us)
Async XLA Ops:
  6.5 93.1 %copy-start.7 = (s32[8,1,64,128]{3,2,1,0:T(8,128)S(1)}, s32[8,1,64,128]{3,2,1,0:T(8,128)}, u32[]{:S(2)}) copy-start(s32[8,1,64,128]{3,2,1,0:T(8,128)} %param.12) | copy-start | bytes 786436
  6.5 564.4 %all-reduce.3.cloned.1.call-start = ((), (), s32[]{:S(2)}) async-start(), calls=%async_computation | async-start | bytes 4194304
  6.5 27.9 %collective-permute-start = (bf16[8,32,4096]{2,1,0:T(8,128)(2,1)}, bf16[8,32,4096]{2,1,0:T(8,128)(2,1)S(1)}, u32[]{:S(2)}, u32[]{:S(2)}) collective-permute-start(bf16[8,32,4096]{2,1,0:T(8,128)(2,1)} %param.8), channel_id=1, source_target_pairs={{0,15},{1,0},{2,1},{3,2},{4,3},{5,4},{6,5},{7,6},{8,7},{9,8},{10,9... | collective-permute-start | bytes 6291464 | tf_op jit(solution)/shard_map/ppermute | solution.py:15
  34.4 29.0 %copy-start.5 = (bf16[8,32,4096]{2,1,0:T(8,128)(2,1)}, bf16[8,32,4096]{2,1,0:T(8,128)(2,1)S(1)}, u32[]{:S(2)}) copy-start(bf16[8,32,4096]{2,1,0:T(8,128)(2,1)S(1)} %collective-permute-done) | copy-start | bytes 6291460
  34.4 29.0 %collective-permute-start.1 = (bf16[8,32,4096]{2,1,0:T(8,128)(2,1)S(1)}, bf16[8,32,4096]{2,1,0:T(8,128)(2,1)S(1)}, u32[]{:S(2)}, u32[]{:S(2)}) collective-permute-start(bf16[8,32,4096]{2,1,0:T(8,128)(2,1)S(1)} %collective-permute-done), channel_id=1, source_target_pairs={{0,15},{1,0},{2,1},{3,2},{4,3},{5,4},{6,5},{7,6},{8,7},{9,8},{10,9... | collective-permute-start | bytes 6291464 | tf_op jit(solution)/shard_map/ppermute | solution.py:15
  63.4 29.1 %copy-start.3 = (bf16[8,32,4096]{2,1,0:T(8,128)(2,1)}, bf16[8,32,4096]{2,1,0:T(8,128)(2,1)S(1)}, u32[]{:S(2)}) copy-start(bf16[8,32,4096]{2,1,0:T(8,128)(2,1)S(1)} %collective-permute-done.1) | copy-start | bytes 6291460
  63.4 29.1 %collective-permute-start.2 = (bf16[8,32,4096]{2,1,0:T(8,128)(2,1)S(1)}, bf16[8,32,4096]{2,1,0:T(8,128)(2,1)S(1)}, u32[]{:S(2)}, u32[]{:S(2)}) collective-permute-start(bf16[8,32,4096]{2,1,0:T(8,128)(2,1)S(1)} %collective-permute-done.1), channel_id=1, source_target_pairs={{0,15},{1,0},{2,1},{3,2},{4,3},{5,4},{6,5},{7,6},{8,7},{9,8},{10,9... | collective-permute-start | bytes 6291464 | tf_op jit(solution)/shard_map/ppermute | solution.py:15
  92.5 15.4 %copy-start.1 = (bf16[8,32,4096]{2,1,0:T(8,128)(2,1)}, bf16[8,32,4096]{2,1,0:T(8,128)(2,1)S(1)}, u32[]{:S(2)}) copy-start(bf16[8,32,4096]{2,1,0:T(8,128)(2,1)S(1)} %collective-permute-done.2) | copy-start | bytes 6291460
  92.5 29.1 %collective-permute-start.3 = (bf16[8,32,4096]{2,1,0:T(8,128)(2,1)S(1)}, bf16[8,32,4096]{2,1,0:T(8,128)(2,1)}, u32[]{:S(2)}, u32[]{:S(2)}) collective-permute-start(bf16[8,32,4096]{2,1,0:T(8,128)(2,1)S(1)} %collective-permute-done.2), channel_id=1, source_target_pairs={{0,15},{1,0},{2,1},{3,2},{4,3},{5,4},{6,5},{7,6},{8,7},{9,8},{10,9... | collective-permute-start | bytes 6291464 | tf_op jit(solution)/shard_map/ppermute | solution.py:15
  99.7 27.5 %copy-start = (bf16[8,32,4096]{2,1,0:T(8,128)(2,1)S(1)}, bf16[8,32,4096]{2,1,0:T(8,128)(2,1)}, u32[]{:S(2)}) copy-start(bf16[8,32,4096]{2,1,0:T(8,128)(2,1)} %param.8) | copy-start | bytes 6291460
  121.6 29.5 %collective-permute-start.4 = (bf16[8,32,4096]{2,1,0:T(8,128)(2,1)}, bf16[8,32,4096]{2,1,0:T(8,128)(2,1)}, u32[]{:S(2)}, u32[]{:S(2)}) collective-permute-start(bf16[8,32,4096]{2,1,0:T(8,128)(2,1)} %collective-permute-done.3), channel_id=1, source_target_pairs={{0,15},{1,0},{2,1},{3,2},{4,3},{5,4},{6,5},{7,6},{8,7},{9,8},{10,9... | collective-permute-start | bytes 6291464 | tf_op jit(solution)/shard_map/ppermute | solution.py:15
  127.2 3.3 copy-start.9
  127.2 3.4 copy-start.10
  130.7 3.5 copy-start.6
  137.7 20.5 %copy-start.4 = (bf16[8,32,4096]{2,1,0:T(8,128)(2,1)S(1)}, bf16[8,32,4096]{2,1,0:T(8,128)(2,1)}, u32[]{:S(2)}) copy-start(bf16[8,32,4096]{2,1,0:T(8,128)(2,1)} %copy-done.3) | copy-start | bytes 6291460
  151.0 29.4 %collective-permute-start.5 = (bf16[8,32,4096]{2,1,0:T(8,128)(2,1)}, bf16[8,32,4096]{2,1,0:T(8,128)(2,1)}, u32[]{:S(2)}, u32[]{:S(2)}) collective-permute-start(bf16[8,32,4096]{2,1,0:T(8,128)(2,1)} %collective-permute-done.4), channel_id=1, source_target_pairs={{0,15},{1,0},{2,1},{3,2},{4,3},{5,4},{6,5},{7,6},{8,7},{9,8},{10,9... | collective-permute-start | bytes 6291464 | tf_op jit(solution)/shard_map/ppermute | solution.py:15
  180.4 29.4 %collective-permute-start.6 = (bf16[8,32,4096]{2,1,0:T(8,128)(2,1)}, bf16[8,32,4096]{2,1,0:T(8,128)(2,1)}, u32[]{:S(2)}, u32[]{:S(2)}) collective-permute-start(bf16[8,32,4096]{2,1,0:T(8,128)(2,1)} %collective-permute-done.5), channel_id=1, source_target_pairs={{0,15},{1,0},{2,1},{3,2},{4,3},{5,4},{6,5},{7,6},{8,7},{9,8},{10,9... | collective-permute-start | bytes 6291464 | tf_op jit(solution)/shard_map/ppermute | solution.py:15
  209.8 29.4 %collective-permute-start.7 = (bf16[8,32,4096]{2,1,0:T(8,128)(2,1)}, bf16[8,32,4096]{2,1,0:T(8,128)(2,1)}, u32[]{:S(2)}, u32[]{:S(2)}) collective-permute-start(bf16[8,32,4096]{2,1,0:T(8,128)(2,1)} %collective-permute-done.6), channel_id=1, source_target_pairs={{0,15},{1,0},{2,1},{3,2},{4,3},{5,4},{6,5},{7,6},{8,7},{9,8},{10,9... | collective-permute-start | bytes 6291464 | tf_op jit(solution)/shard_map/ppermute | solution.py:15
  247.2 18.3 %copy-start.11 = (f32[8]{0:T(128)S(1)}, f32[8]{0:T(128)}, u32[]{:S(2)}) copy-start(f32[8]{0:T(128)} %get-tuple-element.71) | copy-start | bytes 100
  247.2 18.3 %copy-start.12 = (f32[8]{0:T(128)S(1)}, f32[8]{0:T(128)}, u32[]{:S(2)}) copy-start(f32[8]{0:T(128)} %get-tuple-element.72) | copy-start | bytes 100
  247.2 18.3 %copy-start.13 = (f32[8]{0:T(128)S(1)}, f32[8]{0:T(128)}, u32[]{:S(2)}) copy-start(f32[8]{0:T(128)} %get-tuple-element.73) | copy-start | bytes 100
  247.2 18.3 %copy-start.14 = (f32[8]{0:T(128)S(1)}, f32[8]{0:T(128)}, u32[]{:S(2)}) copy-start(f32[8]{0:T(128)} %get-tuple-element.74) | copy-start | bytes 100
  247.3 18.3 %copy-start.15 = (f32[8]{0:T(128)S(1)}, f32[8]{0:T(128)}, u32[]{:S(2)}) copy-start(f32[8]{0:T(128)} %get-tuple-element.75) | copy-start | bytes 100
  247.3 18.3 %copy-start.16 = (s32[8,1,64,128]{3,2,1,0:T(8,128)S(1)}, s32[8,1,64,128]{3,2,1,0:T(8,128)}, u32[]{:S(2)}) copy-start(s32[8,1,64,128]{3,2,1,0:T(8,128)} %param.11) | copy-start | bytes 786436
  (2 other events, 5.7 us)
Sparse Core Ops, SparseCore 0:
  306.0 264.8 all-reduce.2
where the time goes:
time: 581 us; the launch traced here: 579 us
  waiting for transfers between devices  389 us (67%)
  matrix products  59.6 us (10%)
  local copies, waits for them, and re-layouts  47.6 us (8%)
  starting transfers between devices  42.7 us (7%)
  other arithmetic  26.2 us (5%)
  between operations  13.7 us (2%)
    unnamed x2, waiting for transfers between devices  265 us
    ppermute x8, waiting for transfers between devices, from_behind(): return lax.ppermute(value, axis, pairs)  124 us
    ppermute x8, starting transfers between devices, from_behind(): return lax.ppermute(value, axis, pairs)  42.7 us
    dot_general x9, matrix products, correlate(): jnp.einsum('cik,cjk->cij', voltages, paired, preferred_element_type=jnp.f...  24.6 us
    dot_general x8, matrix products, pick_channel(): chosen_rows = jnp.dot(row_hot, table, preferred_element_type=jnp.float32)  15.9 us
    neg x9, other arithmetic, rotate_parts(): -block[..., half_width:]  15.1 us
    transpose x1, local copies, waits for them, and re-layouts, on_device(): jnp.einsum('ctku,ctkrv->ctruv', row_taps, weighted, preferred_element_typ...  13.8 us
    another operation x11, local copies, waits for them, and re-layouts, on_device(): jnp.stack(blocks, axis=1).reshape(n_chan, shifts, n_group, 2, n_group)  13.6 us
  transfers between devices with their start and end apart: 9, of which 9 were waited for; matrix products, arithmetic and copies ran while one was open for 11% of the time, Pallas kernels for 0%

commit v1 on v0

v1 whole, which is shorter than its diff:
```python
import math

import jax
import jax.numpy as jnp
from jax import lax
from jax.experimental import pallas as pl
from jax.experimental.pallas import tpu as pltpu
from jax.sharding import PartitionSpec as P

MESH = pl.DeviceIdType.MESH
TILE = 32
GRP = 32
SAMPLES = 1024
TILES_CH = 64
CAP = 128
GRID_TILES = 256
TAB_ROWS = 40
F32 = jnp.float32
BF16 = jnp.bfloat16


def dot_nt(a, b):
    return lax.dot_general(a, b, (((1,), (1,)), ((), ())), preferred_element_type=F32)


def correlate_kernel(volt, lists, tab, lists_out, xs, neg, gram, got,
                     v_send, v_recv, l_send, l_recv, own_sem, e_send, e_recv):
    chan = lax.axis_index("chan")
    me = lax.axis_index("stn")
    chip = me // 2
    pol = lax.rem(me, 2)

    barrier = pltpu.get_barrier_semaphore()
    for j in range(1, 16):
        pl.semaphore_signal(barrier, 1, device_id=(chan, lax.rem(me + j, 16)), device_id_type=MESH)
    pl.semaphore_wait(barrier, 15)

    def volt_src(dest, half):
        return volt.at[dest // 2, :, pl.ds(pl.multiple_of(half * 2048 + lax.rem(dest, 2) * 1024, 1024), 1024)]

    def volt_dst(half):
        return xs.at[pl.ds(pl.multiple_of(me * GRP, GRP), GRP), pl.ds(half * 1024, 1024)]

    list_core = me // 8
    list_slot = lax.rem(me, 8)

    def list_copy(k):
        return pltpu.make_async_remote_copy(
            lists.at[k], lists_out.at[list_slot], l_send.at[k], l_recv.at[list_slot],
            device_id=(chan, 2 * k + list_core), device_id_type=MESH)

    def list_local(k):
        return pltpu.make_async_copy(lists.at[k], lists_out.at[list_slot], l_recv.at[list_slot])

    for k in range(8):
        @pl.when(2 * k + list_core != me)
        def _():
            list_copy(k).start()

        @pl.when(2 * k + list_core == me)
        def _():
            list_local(k).start()

    copies = []
    for half in range(2):
        for j in range(1, 16):
            dest = lax.rem(me + j, 16)
            copy = pltpu.make_async_remote_copy(
                volt_src(dest, half), volt_dst(half), v_send.at[half, j - 1], v_recv.at[half, j - 1],
                device_id=(chan, dest), device_id_type=MESH)
            copy.start()
            copies.append(copy)
    own = [pltpu.make_async_copy(volt_src(me, half), volt_dst(half), own_sem.at[half]) for half in range(2)]
    for copy in own:
        copy.start()
    for copy in own:
        copy.wait()
    for copy in copies:
        copy.wait()

    def products(block):
        row0 = pl.multiple_of(block * 256, 256)
        neg[:, :1024] = xs[pl.ds(row0, 256), 1024:]
        neg[:, 1024:] = -xs[pl.ds(row0, 256), :1024]
        for col in range(2):
            other = block if col == 0 else 1 - block
            right = xs[pl.ds(pl.multiple_of(other * 256, 256), 256), :]
            gram[block, 0, :, col * 256:(col + 1) * 256] = dot_nt(xs[pl.ds(row0, 256), :], right)
            gram[block, 1, :, col * 256:(col + 1) * 256] = dot_nt(neg[...], right)

    products(1 - pol)
    exchange = pltpu.make_async_remote_copy(
        gram.at[1 - pol], got, e_send, e_recv, device_id=(chan, chip * 2 + 1 - pol), device_id_type=MESH)
    exchange.start()
    products(pol)
    exchange.wait()

    lane = lax.broadcasted_iota(jnp.int32, (GRP, 256), 1)
    row = lax.broadcasted_iota(jnp.int32, (GRP, 256), 0)
    lane8 = lax.broadcasted_iota(jnp.int32, (8, 128), 1)
    for g in range(8):
        for part in range(2):
            rows = slice(g * GRP, (g + 1) * GRP)
            full = (gram[pol, part, rows, :] + got[part, rows, :]) * (1.0 / 64.0)
            if g:
                full = pltpu.roll(full, 512 - g * GRP, 1)
            near = jnp.where(lane == row, 0.0, full[:, :256])
            far = jnp.zeros((8, 128), F32)
            for m in range(4):
                piece = full[m * 8:(m + 1) * 8, 256:384]
                if m:
                    piece = pltpu.roll(piece, m * 32, 1)
                far = jnp.where(lane8 // 32 == m, piece, far)
            far = jnp.where(pol == 0, far, 0.0)
            far = jnp.concatenate([far, jnp.zeros((8, 128), F32)], axis=1)
            tab[g, part * TAB_ROWS:(part + 1) * TAB_ROWS, :] = jnp.concatenate([near, far], axis=0).astype(BF16)

    for k in range(8):
        @pl.when(2 * k + list_core != me)
        def _():
            list_copy(k).wait_send()
    for slot in range(8):
        pltpu.make_async_copy(lists.at[0], lists_out.at[slot], l_recv.at[slot]).wait()


def correlate(voltages, lists):
    return pl.pallas_call(
        correlate_kernel,
        out_shape=(
            jax.ShapeDtypeStruct((8, 2 * TAB_ROWS, 256), BF16),
            jax.ShapeDtypeStruct((8, 3, TILES_CH, CAP), jnp.int16),
        ),
        in_specs=[pl.BlockSpec(memory_space=pl.ANY)] * 2,
        out_specs=(pl.BlockSpec(memory_space=pltpu.VMEM), pl.BlockSpec(memory_space=pltpu.VMEM)),
        scratch_shapes=[
            pltpu.VMEM((512, 2048), BF16),
            pltpu.VMEM((256, 2048), BF16),
            pltpu.VMEM((2, 2, 256, 512), F32),
            pltpu.VMEM((2, 256, 512), F32),
            pltpu.SemaphoreType.DMA((2, 15)),
            pltpu.SemaphoreType.DMA((2, 15)),
            pltpu.SemaphoreType.DMA((8,)),
            pltpu.SemaphoreType.DMA((8,)),
            pltpu.SemaphoreType.DMA((2,)),
            pltpu.SemaphoreType.DMA,
            pltpu.SemaphoreType.DMA,
        ],
        compiler_params=pltpu.CompilerParams(collective_id=0, has_side_effects=True),
        name="correlate",
    )(voltages, lists)


def split_dot(left, right, split_left):
    value = left if split_left else right
    high = value.astype(BF16)
    low = (value - high.astype(F32)).astype(BF16)
    if split_left:
        return (jnp.dot(high, right, preferred_element_type=F32)
                + jnp.dot(low, right, preferred_element_type=F32))
    return (jnp.dot(left, high, preferred_element_type=F32)
            + jnp.dot(left, low, preferred_element_type=F32))


def grid_kernel(kern, owner, tab, lists, grid, his, rows, offs_u, offs_v):
    for g in range(8):
        entry = lists[g, 0].astype(jnp.int32)
        shift = entry >> 10
        i = (entry >> 5) & 31
        j = entry & 31
        far = shift == 8
        his[g] = jnp.where(far, (i >> 3) * 32 + j, (shift & 7) * 32 + j)
        rows[g] = jnp.where(shift > 8, -1, jnp.where(far, 32 + (i & 7), i))
        offs_u[g] = lists[g, 1].astype(jnp.int32)
        offs_v[g] = lists[g, 2].astype(jnp.int32)
    grid[...] = jnp.zeros_like(grid)

    chip = lax.axis_index("stn") // 2
    dist = lax.broadcasted_iota(jnp.int32, (32, 128), 1) % 32 - lax.broadcasted_iota(jnp.int32, (32, 128), 0)
    taps_v = jnp.zeros((32, 128), F32)
    for tap in range(8):
        taps_v = jnp.where(dist == tap, kern[chip, 1, tap], taps_v)
    taps_v = taps_v.astype(BF16)
    ro = lax.broadcasted_iota(jnp.int32, (128, 128), 0)
    co = lax.broadcasted_iota(jnp.int32, (128, 128), 1)
    u = (ro % 8) * 4 + (ro % 64) // 16
    same = (ro // 64 == co // 64) & ((ro // 8) % 2 == (co // 32) % 2)
    dist = jnp.where(same, u - co % 32, -1)
    taps_u = jnp.zeros((128, 128), F32)
    for tap in range(8):
        taps_u = jnp.where(dist == tap, kern[chip, 0, tap], taps_u)
    taps_u = taps_u.astype(BF16)

    hot_ids = lax.broadcasted_iota(jnp.int32, (256, 128), 0)
    row_ids = lax.broadcasted_iota(jnp.int32, (TAB_ROWS, 128), 0)
    cell_ids = lax.broadcasted_iota(jnp.int32, (TILE, 128), 0)
    lane_grp = lax.broadcasted_iota(jnp.int32, (16, 128), 1) // 32

    def pair(tp, carry):
        sums = [None, None]
        for gp in range(4):
            left = [[], []]
            right = [[], []]
            for g in (2 * gp, 2 * gp + 1):
                hot = []
                for a in range(2):
                    hi = his[g, pl.ds(2 * tp + a, 1), :]
                    hot.append(jnp.where(hot_ids == hi, 1.0, 0.0).astype(BF16))
                found = jnp.dot(tab[g], jnp.concatenate(hot, axis=1), preferred_element_type=F32)
                for a in range(2):
                    lanes = slice(a * 128, (a + 1) * 128)
                    at_row = row_ids == rows[g, pl.ds(2 * tp + a, 1), :]
                    at_u = cell_ids == offs_u[g, pl.ds(2 * tp + a, 1), :]
                    at_v = cell_ids == offs_v[g, pl.ds(2 * tp + a, 1), :]
                    both = []
                    for part in range(2):
                        block = found[part * TAB_ROWS:(part + 1) * TAB_ROWS, lanes]
                        value = jnp.sum(jnp.where(at_row, block, 0.0), axis=0, keepdims=True)
                        both.append(jnp.where(at_u, value, 0.0))
                    left[a].append(jnp.concatenate(both, axis=0).astype(BF16))
                    right[a].append(jnp.where(at_v, 1.0, 0.0).astype(BF16))
            for a in range(2):
                term = dot_nt(jnp.concatenate(left[a], axis=1), jnp.concatenate(right[a], axis=1))
                sums[a] = term if sums[a] is None else sums[a] + term
        spread = split_dot(jnp.concatenate(sums, axis=0), taps_v, True)
        cells = split_dot(taps_u, spread, False)
        for a in range(2):
            tile = cells[a * 64:a * 64 + 16]
            for ul in range(1, 4):
                tile = jnp.where(lane_grp == ul, cells[a * 64 + ul * 16:a * 64 + ul * 16 + 16], tile)
            where = owner[chip, 2 * tp + a]
            grid[where] = grid[where] + tile
        return carry

    lax.fori_loop(0, TILES_CH // 2, pair, 0)


def grid_local(kern, owner, tab, lists):
    return pl.pallas_call(
        grid_kernel,
        out_shape=jax.ShapeDtypeStruct((GRID_TILES, 16, 128), F32),
        in_specs=[pl.BlockSpec(memory_space=pltpu.SMEM)] * 2 + [pl.BlockSpec(memory_space=pltpu.VMEM)] * 2,
        out_specs=pl.BlockSpec(memory_space=pltpu.VMEM),
        scratch_shapes=[pltpu.VMEM((8, TILES_CH, CAP), jnp.int32)] * 4,
        name="grid_local",
    )(kern, owner, tab, lists)


def reduce_kernel(part, out, got_c, send_a, send_b, got_a, got_b, sum_a, sum_b, got_a2, got_b2, sum_z, got_z,
                  sem_c, s_a, r_a, s_b, r_b, s_a2, r_a2, s_b2, r_b2, s_z, r_z):
    chan = lax.axis_index("chan")
    stn = lax.axis_index("stn")
    z, xlo = chan // 2, lax.rem(chan, 2)
    xhi, y, core = stn // 8, lax.rem(stn // 2, 4), lax.rem(stn, 2)
    x = xhi * 2 + xlo

    def device(x_, y_, z_, core_):
        return (z_ * 2 + lax.rem(x_, 2), (x_ // 2) * 8 + y_ * 2 + core_)

    def slot_x(x_):
        return lax.rem(x_, 2) * 2 + x_ // 2

    def peer_x(d):
        return lax.rem(x + d, 4)

    def peer_y(d):
        return lax.rem(y + d, 4)

    def peer_z(d):
        return lax.rem(z + d, 8)

    peers = [device(x, y, z, 1 - core)]
    peers += [device(peer_x(d), y, z, core) for d in range(1, 4)]
    peers += [device(x, peer_y(d), z, core) for d in range(1, 4)]
    peers += [device(x, y, peer_z(d), core) for d in range(1, 8)]
    barrier = pltpu.get_barrier_semaphore()
    for peer in peers:
        pl.semaphore_signal(barrier, 1, device_id=peer, device_id_type=MESH)
    pl.semaphore_wait(barrier, len(peers))

    def send(src, dst, ss, rs, peer):
        copy = pltpu.make_async_remote_copy(src, dst, ss, rs, device_id=peer, device_id_type=MESH)
        copy.start()
        return copy

    send(part.at[:, 1 - core], got_c, sem_c.at[0], sem_c.at[1], peers[0]).wait()

    def fold(n, carry):
        zq, xs = n // 4, lax.rem(n, 4)
        for yy in range(4):
            m = zq * 16 + xs * 4 + yy
            send_a[yy, n] = (part[m, core] + got_c[m]).astype(BF16)
            send_b[xs, zq * 4 + yy] = (part[64 + m, core] + got_c[64 + m]).astype(BF16)
        return carry

    lax.fori_loop(0, 16, fold, 0)
    first = []
    for d in range(1, 4):
        first.append(send(send_a.at[peer_y(d)], got_a.at[d - 1], s_a.at[d - 1], r_a.at[d - 1],
                          device(x, peer_y(d), z, core)))
        first.append(send(send_b.at[slot_x(peer_x(d))], got_b.at[d - 1], s_b.at[d - 1], r_b.at[d - 1],
                          device(peer_x(d), y, z, core)))
    for copy in first:
        copy.wait()

    def total_a(n, carry):
        m = n * 4 + y
        value = part[m, core] + got_c[m]
        for d in range(3):
            value = value + got_a[d, n].astype(F32)
        sum_a[lax.rem(n, 4), n // 4] = value
        zq, yy = n // 4, lax.rem(n, 4)
        m = 64 + zq * 16 + slot_x(x) * 4 + yy
        value = part[m, core] + got_c[m]
        for d in range(3):
            value = value + got_b[d, n].astype(F32)
        sum_b[yy, zq] = value
        return carry

    lax.fori_loop(0, 16, total_a, 0)
    second = []
    for d in range(1, 4):
        second.append(send(sum_a.at[slot_x(peer_x(d))], got_a2.at[d - 1], s_a2.at[d - 1], r_a2.at[d - 1],
                           device(peer_x(d), y, z, core)))
        second.append(send(sum_b.at[peer_y(d)], got_b2.at[d - 1], s_b2.at[d - 1], r_b2.at[d - 1],
                           device(x, peer_y(d), z, core)))
    for copy in second:
        copy.wait()
    sum_z[0:4] = sum_a[slot_x(x)] + got_a2[0] + got_a2[1] + got_a2[2]
    sum_z[4:8] = sum_b[y] + got_b2[0] + got_b2[1] + got_b2[2]
    third = []
    for d in range(1, 8):
        third.append(send(sum_z.at[peer_z(d)], got_z.at[d - 1], s_z.at[d - 1], r_z.at[d - 1],
                          device(x, y, peer_z(d), core)))
    for copy in third:
        copy.wait()
    value = sum_z[z]
    for d in range(7):
        value = value + got_z[d]
    out[...] = value


def reduce_grid(part):
    dma = pltpu.SemaphoreType.DMA
    return pl.pallas_call(
        reduce_kernel,
        out_shape=jax.ShapeDtypeStruct((16, 128), F32),
        in_specs=[pl.BlockSpec(memory_space=pltpu.VMEM)],
        out_specs=pl.BlockSpec(memory_space=pltpu.VMEM),
        scratch_shapes=[
            pltpu.VMEM((128, 16, 128), F32),
            pltpu.VMEM((4, 16, 16, 128), BF16),
            pltpu.VMEM((4, 16, 16, 128), BF16),
            pltpu.VMEM((3, 16, 16, 128), BF16),
            pltpu.VMEM((3, 16, 16, 128), BF16),
            pltpu.VMEM((4, 4, 16, 128), F32),
            pltpu.VMEM((4, 4, 16, 128), F32),
            pltpu.VMEM((3, 4, 16, 128), F32),
            pltpu.VMEM((3, 4, 16, 128), F32),
            pltpu.VMEM((8, 16, 128), F32),
            pltpu.VMEM((7, 16, 128), F32),
            dma((2,)),
            dma((3,)), dma((3,)), dma((3,)), dma((3,)),
            dma((3,)), dma((3,)), dma((3,)), dma((3,)),
            dma((7,)), dma((7,)),
        ],
        compiler_params=pltpu.CompilerParams(collective_id=1, has_side_effects=True),
        name="reduce_grid",
    )(part.reshape(128, 2, 16, 128))


def on_device(voltages, kernels, tile_lists, offset_u, offset_v, owner_map):
    lists = jnp.stack([tile_lists[:, 0], offset_u[:, 0], offset_v[:, 0]], axis=1).astype(jnp.int16)
    tab, lists_here = correlate(voltages, lists)
    part = grid_local(kernels.astype(F32), owner_map, tab, lists_here)
    return reduce_grid(part).reshape(1, -1)


def solution(mesh):
    placed = (
        P("chan", "stn", None),
        P("chan", None, None),
        P("chan", "stn", None, None),
        P("chan", "stn", None, None),
        P("chan", "stn", None, None),
        P("chan", None),
    )
    return jax.shard_map(
        on_device, mesh=mesh, in_specs=placed, out_specs=P(("chan", "stn"), None), check_vma=False
    )
```

time: 581 us -> 116 us (0.20)
  waiting for transfers between devices: 389 us -> 0 us
  Pallas kernels: 0 us -> 108 us
  matrix products: 59.6 us -> 0 us
  local copies, waits for them, and re-layouts: 47.6 us -> 1.3 us
  starting transfers between devices: 42.7 us -> 0 us
  other arithmetic: 26.2 us -> 4.96 us
  between operations: 13.7 us -> 0.03 us
    unnamed x2 -> x0, waiting for transfers between devices: 265 us -> none
    ppermute x8 -> x0, waiting for transfers between devices: 124 us -> none  [from_behind(): return lax.ppermute(value, axis, pairs)]
    pallas_call x0 -> x3, Pallas kernels: none -> 108 us  [the longest x1 42.3 us: correlate(): pl.pallas_call(correlate_kernel, out_shape=(jax.ShapeDtypeStruct((8, 2 *...]
    dot_general x19 -> x0, matrix products: 59.6 us -> none  [the longest x9 24.6 us: correlate(): jnp.einsum('cik,cjk->cij', voltages, paired, preferred_element_type=jnp.f...]
    ppermute x8 -> x0, starting transfers between devices: 42.7 us -> none  [from_behind(): return lax.ppermute(value, axis, pairs)]
    neg x9 -> x0, other arithmetic: 15.1 us -> none  [rotate_parts(): -block[..., half_width:]]
    transpose x1 -> x0, local copies, waits for them, and re-layouts: 13.8 us -> none  [on_device(): jnp.einsum('ctku,ctkrv->ctruv', row_taps, weighted, preferred_element_typ...]
    another operation x11 -> x0, local copies, waits for them, and re-layouts: 13.6 us -> none  [on_device(): jnp.stack(blocks, axis=1).reshape(n_chan, shifts, n_group, 2, n_group)]
  transfers between devices with their start and end apart: 9 -> 0, of which waited for: 9 -> 0; matrix products, arithmetic and copies ran while one was open for 11% -> 0% of each run, Pallas kernels for 0% -> 0%
where the time goes in v1:
time: 116 us; the launch traced here: 114 us
  Pallas kernels  108 us (93%)
  other arithmetic  4.96 us (4%)
  local copies, waits for them, and re-layouts  1.3 us (1%)
    pallas_call x1, Pallas kernels, correlate(): pl.pallas_call(correlate_kernel, out_shape=(jax.ShapeDtypeStruct((8, 2 *...  42.3 us
    pallas_call x1, Pallas kernels, grid_local(): pl.pallas_call(grid_kernel, out_shape=jax.ShapeDtypeStruct((GRID_TILES, 1...  37.2 us
    pallas_call x1, Pallas kernels, reduce_grid(): pl.pallas_call(reduce_kernel, out_shape=jax.ShapeDtypeStruct((16, 128), F...  28.6 us
    another operation x3, other arithmetic  2.91 us

profile of v1, /device:TPU:2, one launch (start us, length us, event | category | flops | bytes accessed | tf_op | source)
XLA Modules:
  0.0 114.4 jit_solution(17044187591204288675)
XLA Ops:
  0.0 1.3 %convert_element_type.4.kern = f32[8,2,8]{2,1,0:T(2,128)} convert(bf16[8,2,8]{2,1,0:T(2,128)(2,1)} %param.7) | non-fusion elementwise | flops 128 | bytes 768 | tf_op jit(solution)/shard_map/convert_element_type | solution.py:374
  1.3 1.0 convert.9
  2.3 1.0 convert.10
  3.2 1.0 convert.11
  4.2 0.8 pad_add_fusion.lists
  5.0 42.3 %correlate.1 = (bf16[8,80,256]{2,1,0:T(8,128)(2,1)}, s16[8,3,64,128]{3,2,1,0:T(8,128)(2,1)}) custom-call(bf16[8,32,4096]{2,1,0:T(8,128)(2,1)} %volt.1, s16[8,3,64,128]{3,2,1,0:T(8,128)(2,1)} %pad_add_fusion.lists), custom_call_target="tpu_custom_call" | custom-call | tf_op jit(solution)/shard_map/correlate/pallas_call | solution.py:127
  47.3 37.2 %grid_local.1 = f32[256,16,128]{2,1,0:T(8,128)} custom-call(f32[8,2,8]{2,1,0:T(2,128)} %convert_element_type.4.kern, s32[8,64]{1,0:T(8,128)} %owner.1, bf16[8,80,256]{2,1,0:T(8,128)(2,1)} %get-tuple-element.7.tab, s16[8,3,64,128]{3,2,1,0:T(8,128)(2,1)} %get-tuple-element.8.lists), custom_call_target="tpu_custom_call" | custom-call | tf_op jit(solution)/shard_map/grid_local/pallas_call | solution.py:238
  84.5 28.6 %reduce_grid.1 = f32[16,128]{1,0:T(8,128)} custom-call(f32[128,2,16,128]{3,2,1,0:T(8,128)} %bitcast.2), custom_call_target="tpu_custom_call" | custom-call | tf_op jit(solution)/shard_map/reduce_grid/pallas_call | solution.py:344
  113.1 1.3 %copy.8 = f32[1,2048]{1,0:T(1,128)} copy(f32[1,2048]{1,0:T(1,128)} %bitcast.3) | data formatting | bytes 16384

commit v2 on v0

v2 whole, which is shorter than its diff:
```python
import math

import jax
import jax.numpy as jnp
from jax import lax
from jax.experimental import pallas as pl
from jax.experimental.pallas import tpu as pltpu
from jax.sharding import PartitionSpec as P

MESH = pl.DeviceIdType.MESH
TILE = 32
GRP = 32
SAMPLES = 1024
TILES_CH = 64
CAP = 128
GRID_TILES = 256
TAB_ROWS = 80
N_CHIPS = 8
F32 = jnp.float32
BF16 = jnp.bfloat16


def dot_nt(a, b):
    return lax.dot_general(a, b, (((1,), (1,)), ((), ())), preferred_element_type=F32)


def chan_kernel(volt, entries, off_u_in, off_v_in, kern, owner, out,
                xs, neg, gram, got, raw, packed, lists, tab, his, rows, offs_u, offs_v, buf0, buf1, sums,
                mine, theirs, dense, send_a, send_b, got_a, got_b, sum_a, sum_b, got_a2, got_b2, sum_z, got_z,
                raw_sem, v_send, v_recv, l_send, l_recv, own_sem, e_sem, t_send, t_recv,
                s_a, r_a, s_b, r_b, s_a2, r_a2, s_b2, r_b2, s_z, r_z):
    chan = lax.axis_index("chan")
    me = lax.axis_index("stn")
    chip = me // 2
    core = lax.rem(me, 2)
    z, xlo = chan // 2, lax.rem(chan, 2)
    xhi, y = me // 8, lax.rem(chip, 4)
    x = xhi * 2 + xlo

    def device(x_, y_, z_):
        return (z_ * 2 + lax.rem(x_, 2), (x_ // 2) * 8 + y_ * 2 + core)

    def slot_x(x_):
        return lax.rem(x_, 2) * 2 + x_ // 2

    def peer_x(d):
        return lax.rem(x + d, 4)

    def peer_y(d):
        return lax.rem(y + d, 4)

    def peer_z(d):
        return lax.rem(z + d, 8)

    partner = (chan, 2 * chip + 1 - core)
    peers = [(chan, lax.rem(me + j, 16)) for j in range(1, 16)]
    peers += [device(peer_x(d), y, z) for d in (1, 3)]
    peers += [device(x, y, peer_z(d)) for d in range(1, 8)]
    barrier = pltpu.get_barrier_semaphore()
    for peer in peers:
        pl.semaphore_signal(barrier, 1, device_id=peer, device_id_type=MESH)

    loads = [pltpu.make_async_copy(ref.at[:, 0], raw.at[n], raw_sem.at[n])
             for n, ref in enumerate((entries, off_u_in, off_v_in))]
    for copy in loads:
        copy.start()
    for copy in loads:
        copy.wait()

    def narrow(k, carry):
        for n in range(3):
            packed[k, n] = raw[n, k].astype(jnp.int16)
        return carry

    lax.fori_loop(0, N_CHIPS, narrow, 0)
    pl.semaphore_wait(barrier, len(peers))

    def send(src, dst, ss, rs, peer):
        copy = pltpu.make_async_remote_copy(src, dst, ss, rs, device_id=peer, device_id_type=MESH)
        copy.start()
        return copy

    list_core = me // 8
    list_slot = lax.rem(me, 8)

    def list_copy(k):
        return pltpu.make_async_remote_copy(
            packed.at[k], lists.at[list_slot], l_send.at[k], l_recv.at[list_slot],
            device_id=(chan, 2 * k + list_core), device_id_type=MESH)

    for k in range(N_CHIPS):
        @pl.when(2 * k + list_core != me)
        def _():
            list_copy(k).start()

        @pl.when(2 * k + list_core == me)
        def _():
            pltpu.make_async_copy(packed.at[k], lists.at[list_slot], l_recv.at[list_slot]).start()

    def volt_src(dest, half):
        return volt.at[dest // 2, :, pl.ds(pl.multiple_of(half * 2048 + lax.rem(dest, 2) * 1024, 1024), 1024)]

    def volt_dst(half):
        return xs.at[pl.ds(pl.multiple_of(me * GRP, GRP), GRP), pl.ds(half * 1024, 1024)]

    copies = []
    for half in range(2):
        for j in range(1, 16):
            dest = lax.rem(me + j, 16)
            copies.append(send(volt_src(dest, half), volt_dst(half), v_send.at[half, j - 1],
                               v_recv.at[half, j - 1], (chan, dest)))
    own = [pltpu.make_async_copy(volt_src(me, half), volt_dst(half), own_sem.at[half]) for half in range(2)]
    for copy in own:
        copy.start()

    for slot in range(8):
        pltpu.make_async_copy(packed.at[0], lists.at[slot], l_recv.at[slot]).wait()

    def prepare(g, carry):
        entry = lists[g, 0].astype(jnp.int32)
        shift = entry >> 10
        i = (entry >> 5) & 31
        j = entry & 31
        far = shift == 8
        his[g] = jnp.where(far, (i >> 3) * 32 + j, (shift & 7) * 32 + j)
        rows[g] = jnp.where(shift > 8, -1, jnp.where(far, 32 + (i & 7), i))
        offs_u[g] = lists[g, 1].astype(jnp.int32)
        offs_v[g] = lists[g, 2].astype(jnp.int32)
        return carry

    lax.fori_loop(0, 8, prepare, 0)
    iota = lambda shape, axis: lax.broadcasted_iota(jnp.int32, shape, axis)
    taps = kern[chip].astype(F32)
    dist = iota((64, 128), 1) % 32 - iota((64, 128), 0) % 32
    taps_v = jnp.zeros((64, 128), F32)
    for tap in range(8):
        taps_v = jnp.where(dist == tap, taps[1:2, tap:tap + 1], taps_v)
    taps_v = taps_v.astype(BF16)
    ro, co = iota((128, 128), 0), iota((128, 128), 1)
    u = (ro % 8) * 4 + (ro % 64) // 16
    same = (ro // 64 == co // 64) & ((ro // 8) % 2 == (co // 32) % 2)
    dist = jnp.where(same, u - co % 32, -1)
    taps_u = jnp.zeros((128, 128), F32)
    for tap in range(8):
        taps_u = jnp.where(dist == tap, taps[0:1, tap:tap + 1], taps_u)
    taps_u = taps_u.astype(BF16)
    taps_u = jnp.concatenate([taps_u, taps_u], axis=1)
    low = ro % 64
    outer, inner, zq = low // 16, (low // 4) % 4, low % 4
    ys = jnp.where(ro < 64, outer, inner)
    xslot = jnp.where(ro < 64, inner, outer)
    cell = (zq + 4 * (ro // 64)) * 32 + xslot * 8 + ys * 2 + core
    owners = owner[pl.ds(chip, 1), :]
    owners = jnp.concatenate([owners, owners], axis=1)
    owner_hot = jnp.where(cell == owners, 1.0, 0.0).astype(BF16)
    ro, co = iota((64, 48), 0), iota((64, 48), 1)
    spread_ones = jnp.where(jnp.where(co < 32, co // 16, (co - 32) // 8) == ro // 32, 1.0, 0.0).astype(BF16)

    for copy in own:
        copy.wait()
    for copy in copies:
        copy.wait()

    def products(block):
        row0 = pl.multiple_of(block * 256, 256)
        neg[:, :1024] = xs[pl.ds(row0, 256), 1024:]
        neg[:, 1024:] = -xs[pl.ds(row0, 256), :1024]
        for col in range(2):
            other = block if col == 0 else 1 - block
            right = xs[pl.ds(pl.multiple_of(other * 256, 256), 256), :]
            gram[block, 0, :, col * 256:(col + 1) * 256] = dot_nt(xs[pl.ds(row0, 256), :], right)
            gram[block, 1, :, col * 256:(col + 1) * 256] = dot_nt(neg[...], right)

    products(1 - core)
    exchange = send(gram.at[1 - core], got, e_sem.at[0], e_sem.at[1], partner)
    products(core)
    exchange.wait()

    lane, row = iota((GRP, 256), 1), iota((GRP, 256), 0)
    lane_grp8 = iota((8, 128), 1) // 32
    for g in range(8):
        fars = []
        for part in range(2):
            block = slice(g * GRP, (g + 1) * GRP)
            full = (gram[core, part, block, :] + got[part, block, :]) * (1.0 / 64.0)
            if g:
                full = pltpu.roll(full, 512 - g * GRP, 1)
            near = jnp.where(lane == row, 0.0, full[:, :256])
            tab[g, part * GRP:(part + 1) * GRP, :] = near.astype(BF16)
            far = jnp.zeros((8, 128), F32)
            for m in range(4):
                piece = full[m * 8:(m + 1) * 8, 256:384]
                if m:
                    piece = pltpu.roll(piece, m * 32, 1)
                far = jnp.where(lane_grp8 == m, piece, far)
            fars.append(jnp.where(core == 0, far, 0.0))
        far = jnp.concatenate(fars, axis=0)
        tab[g, 64:80, :] = jnp.concatenate([far, jnp.zeros((16, 128), F32)], axis=1).astype(BF16)

    ids16 = iota((16, 128), 0).astype(jnp.int16)
    hot_ids = [(iota((16, 128), 0) + 16 * n).astype(jnp.int16) for n in range(16)]
    far_ids = (iota((16, 128), 0) % 8 + 32).astype(jnp.int16)
    one, zero = jnp.ones((), BF16), jnp.zeros((), BF16)

    def line(ref, g, t):
        return jnp.broadcast_to(ref[g, pl.ds(t, 1), :], (16, 128)).astype(jnp.int16)

    def fetch(tp, buf, g):
        hot = []
        for a in range(2):
            hi = line(his, g, 2 * tp + a)
            hot.append(jnp.concatenate([jnp.where(ids == hi, one, zero) for ids in hot_ids], axis=0))
        buf[g] = jnp.dot(tab[g], jnp.concatenate(hot, axis=1), preferred_element_type=F32).astype(BF16)

    def place(tp, buf, g, left, right):
        picked = []
        for a in range(2):
            r = line(rows, g, 2 * tp + a)
            near, mid, far = ids16 == r, hot_ids[1] == r, far_ids == r
            lanes = slice(a * 128, (a + 1) * 128)
            tiles = [buf[g, n * 16:(n + 1) * 16, lanes] for n in range(5)]
            re = jnp.where(near, tiles[0], jnp.where(mid, tiles[1], zero))
            im = jnp.where(near, tiles[2], jnp.where(mid, tiles[3], zero))
            picked.append(jnp.concatenate([re, im, jnp.where(far, tiles[4], zero)], axis=0))
        wide = jnp.dot(spread_ones, jnp.concatenate(picked, axis=1), preferred_element_type=F32).astype(BF16)
        for a in range(2):
            lanes = slice(a * 128, (a + 1) * 128)
            at_u = line(offs_u, g, 2 * tp + a)
            at_v = line(offs_v, g, 2 * tp + a)
            masks = [ids16 == at_u, hot_ids[1] == at_u]
            left[a].append(jnp.concatenate(
                [jnp.where(masks[n % 2], wide[n * 16:(n + 1) * 16, lanes], zero) for n in range(4)], axis=0))
            right[a].append(jnp.concatenate(
                [jnp.where(ids == at_v, one, zero) for ids in (ids16, hot_ids[1])], axis=0))

    def stage(tp_next, buf_next, tp, buf):
        totals = [None, None]
        for gp in range(4):
            left, right = [[], []], [[], []]
            for g in (2 * gp, 2 * gp + 1):
                fetch(tp_next, buf_next, g)
                place(tp, buf, g, left, right)
            for a in range(2):
                twice = jnp.concatenate(right[a], axis=1)
                term = dot_nt(jnp.concatenate(left[a], axis=1), jnp.concatenate([twice, twice], axis=0))
                totals[a] = term if totals[a] is None else totals[a] + term
        for a in range(2):
            sums[2 * tp + a] = totals[a]

    for g in range(8):
        fetch(0, buf0, g)

    def pair(i, carry):
        stage(2 * i + 1, buf1, 2 * i, buf0)
        stage(lax.rem(2 * i + 2, TILES_CH // 2), buf0, 2 * i + 1, buf1)
        return carry

    lax.fori_loop(0, TILES_CH // 4, pair, 0)

    first_lanes = iota((128, 64), 1) < 32
    lane_grp = iota((16, 128), 1) // 32

    def tile_copy(step):
        part = pl.ds(pl.multiple_of(step * 8, 8), 8)
        return pltpu.make_async_remote_copy(mine.at[:, part], theirs.at[:, part], t_send.at[step], t_recv.at[step],
                                            device_id=partner, device_id_type=MESH)

    def finish(step, carry):
        for b in range(4):
            t = step * 8 + b * 2
            value = sums[pl.ds(t, 2)].reshape(128, 64)
            high = value.astype(BF16).astype(F32)
            mixed = jnp.where(first_lanes, high, value - high).astype(BF16)
            spread = jnp.dot(mixed, taps_v, preferred_element_type=F32)
            high = spread.astype(BF16)
            low_part = (spread - high.astype(F32)).astype(BF16)
            cells = jnp.dot(taps_u, jnp.concatenate([high, low_part], axis=0), preferred_element_type=F32)
            for a in range(2):
                tile = cells[a * 64:a * 64 + 16]
                for ul in range(1, 4):
                    tile = jnp.where(lane_grp == ul, cells[a * 64 + ul * 16:a * 64 + ul * 16 + 16], tile)
                mine.reshape(16 * TILES_CH, 128)[pl.ds(t + a, 16, stride=TILES_CH), :] = tile
        tile_copy(step).start()
        return carry

    lax.fori_loop(0, TILES_CH // 8, finish, 0)
    for step in range(TILES_CH // 8):
        tile_copy(step).wait()

    for a in range(16):
        value = mine[a] + theirs[a]
        high = value.astype(BF16)
        low_part = (value - high.astype(F32)).astype(BF16)
        cells = jnp.dot(owner_hot, jnp.concatenate([high, low_part], axis=0), preferred_element_type=F32)
        dense[a] = cells
        for n in range(4):
            send_a[n, a] = cells[n * 16:(n + 1) * 16].astype(BF16)
            send_b[n, a] = cells[64 + n * 16:64 + (n + 1) * 16].astype(BF16)

    first = []
    for d in (2, 1, 3):
        first.append(send(send_a.at[peer_y(d)], got_a.at[d - 1], s_a.at[d - 1], r_a.at[d - 1],
                          device(x, peer_y(d), z)))
        first.append(send(send_b.at[slot_x(peer_x(d))], got_b.at[d - 1], s_b.at[d - 1], r_b.at[d - 1],
                          device(peer_x(d), y, z)))
    for copy in first:
        copy.wait()
    at_a = pl.ds(pl.multiple_of(y * 16, 16), 16)
    at_b = pl.ds(pl.multiple_of(64 + slot_x(x) * 16, 16), 16)
    for a in range(16):
        value = dense[a, at_a, :]
        for d in range(3):
            value = value + got_a[d, a].astype(F32)
        sum_a.reshape(256, 128)[pl.ds(a, 16, stride=16), :] = value
        value = dense[a, at_b, :]
        for d in range(3):
            value = value + got_b[d, a].astype(F32)
        sum_b.reshape(256, 128)[pl.ds(a, 16, stride=16), :] = value

    def four(slot):
        return pl.ds(pl.multiple_of(slot * 4, 4), 4)

    second = []
    for d in (2, 1, 3):
        second.append(send(sum_a.at[four(slot_x(peer_x(d)))], got_a2.at[d - 1], s_a2.at[d - 1], r_a2.at[d - 1],
                           device(peer_x(d), y, z)))
        second.append(send(sum_b.at[four(peer_y(d))], got_b2.at[d - 1], s_b2.at[d - 1], r_b2.at[d - 1],
                           device(x, peer_y(d), z)))
    for copy in second:
        copy.wait()
    sum_z[0:4] = sum_a[four(slot_x(x))] + got_a2[0] + got_a2[1] + got_a2[2]
    sum_z[4:8] = sum_b[four(y)] + got_b2[0] + got_b2[1] + got_b2[2]
    third = []
    for d in (4, 3, 5, 2, 6, 1, 7):
        third.append(send(sum_z.at[peer_z(d)], got_z.at[d - 1], s_z.at[d - 1], r_z.at[d - 1],
                          device(x, y, peer_z(d))))
    for k in range(N_CHIPS):
        @pl.when(2 * k + list_core != me)
        def _():
            list_copy(k).wait_send()
    for copy in third:
        copy.wait()
    value = sum_z[z]
    for d in range(7):
        value = value + got_z[d]
    for n in range(16):
        out[:, n * 128:(n + 1) * 128] = value[n:n + 1]


def on_device(voltages, kernels, tile_lists, offset_u, offset_v, owner_map):
    dma = pltpu.SemaphoreType.DMA
    anywhere, vmem = pl.BlockSpec(memory_space=pl.ANY), pl.BlockSpec(memory_space=pltpu.VMEM)
    lists_shape = (8, 3, TILES_CH, CAP)
    return pl.pallas_call(
        chan_kernel,
        out_shape=jax.ShapeDtypeStruct((1, 2048), F32),
        in_specs=[anywhere] * 4 + [vmem] * 2,
        out_specs=vmem,
        scratch_shapes=[
            pltpu.VMEM((512, 2048), BF16),
            pltpu.VMEM((256, 2048), BF16),
            pltpu.VMEM((2, 2, 256, 512), F32),
            pltpu.VMEM((2, 256, 512), F32),
            pltpu.VMEM((3, 8, TILES_CH, CAP), jnp.int32),
            pltpu.VMEM(lists_shape, jnp.int16),
            pltpu.VMEM(lists_shape, jnp.int16),
            pltpu.VMEM((8, TAB_ROWS, 256), BF16),
        ] + [pltpu.VMEM((8, TILES_CH, CAP), jnp.int32)] * 4 + [pltpu.VMEM((8, TAB_ROWS, 256), BF16)] * 2 + [
            pltpu.VMEM((TILES_CH, 64, 64), F32),
            pltpu.VMEM((16, TILES_CH, 128), F32),
            pltpu.VMEM((16, TILES_CH, 128), F32),
            pltpu.VMEM((16, 128, 128), F32),
            pltpu.VMEM((4, 16, 16, 128), BF16),
            pltpu.VMEM((4, 16, 16, 128), BF16),
            pltpu.VMEM((3, 16, 16, 128), BF16),
            pltpu.VMEM((3, 16, 16, 128), BF16),
            pltpu.VMEM((16, 16, 128), F32),
            pltpu.VMEM((16, 16, 128), F32),
            pltpu.VMEM((3, 4, 16, 128), F32),
            pltpu.VMEM((3, 4, 16, 128), F32),
            pltpu.VMEM((8, 16, 128), F32),
            pltpu.VMEM((7, 16, 128), F32),
            dma((3,)), dma((2, 15)), dma((2, 15)), dma((8,)), dma((8,)), dma((2,)), dma((2,)), dma((8,)), dma((8,)),
            dma((3,)), dma((3,)), dma((3,)), dma((3,)),
            dma((3,)), dma((3,)), dma((3,)), dma((3,)),
            dma((7,)), dma((7,)),
        ],
        compiler_params=pltpu.CompilerParams(collective_id=0, has_side_effects=True),
        name="correlate_and_grid",
    )(voltages, tile_lists, offset_u, offset_v, kernels, owner_map)


def solution(mesh):
    placed = (
        P("chan", "stn", None),
        P("chan", None, None),
        P("chan", "stn", None, None),
        P("chan", "stn", None, None),
        P("chan", "stn", None, None),
        P("chan", None),
    )
    return jax.shard_map(
        on_device, mesh=mesh, in_specs=placed, out_specs=P(("chan", "stn"), None), check_vma=False
    )
```

time: 581 us -> 92.8 us (0.16)
  waiting for transfers between devices: 389 us -> 0 us
  Pallas kernels: 0 us -> 91.3 us
  matrix products: 59.6 us -> 0 us
  local copies, waits for them, and re-layouts: 47.6 us -> 1.3 us
  starting transfers between devices: 42.7 us -> 0 us
  other arithmetic: 26.2 us -> 0 us
  between operations: 13.7 us -> 0.01 us
    unnamed x2 -> x0, waiting for transfers between devices: 265 us -> none
    ppermute x8 -> x0, waiting for transfers between devices: 124 us -> none  [from_behind(): return lax.ppermute(value, axis, pairs)]
    pallas_call x0 -> x1, Pallas kernels: none -> 91.3 us  [on_device(): pl.pallas_call(chan_kernel, out_shape=jax.ShapeDtypeStruct((1, 2048), F32...]
    dot_general x19 -> x0, matrix products: 59.6 us -> none  [the longest x9 24.6 us: correlate(): jnp.einsum('cik,cjk->cij', voltages, paired, preferred_element_type=jnp.f...]
    ppermute x8 -> x0, starting transfers between devices: 42.7 us -> none  [from_behind(): return lax.ppermute(value, axis, pairs)]
    neg x9 -> x0, other arithmetic: 15.1 us -> none  [rotate_parts(): -block[..., half_width:]]
    transpose x1 -> x0, local copies, waits for them, and re-layouts: 13.8 us -> none  [on_device(): jnp.einsum('ctku,ctkrv->ctruv', row_taps, weighted, preferred_element_typ...]
    another operation x11 -> x0, local copies, waits for them, and re-layouts: 13.6 us -> none  [on_device(): jnp.stack(blocks, axis=1).reshape(n_chan, shifts, n_group, 2, n_group)]
  transfers between devices with their start and end apart: 9 -> 0, of which waited for: 9 -> 0; matrix products, arithmetic and copies ran while one was open for 11% -> 0% of each run, Pallas kernels for 0% -> 0%
where the time goes in v2:
time: 92.8 us; the launch traced here: 92.6 us
  Pallas kernels  91.3 us (98%)
  local copies, waits for them, and re-layouts  1.3 us (1%)
    pallas_call x1, Pallas kernels, on_device(): pl.pallas_call(chan_kernel, out_shape=jax.ShapeDtypeStruct((1, 2048), F32...  91.3 us

profile of v2, /device:TPU:2, one launch (start us, length us, event | category | flops | bytes accessed | tf_op | source)
XLA Modules:
  0.0 92.6 jit_solution(5256705615100003063)
XLA Ops:
  0.0 91.3 %correlate_and_grid.1 = f32[1,2048]{1,0:T(1,128)} custom-call(bf16[8,32,4096]{2,1,0:T(8,128)(2,1)} %volt.1, s32[8,1,64,128]{3,2,1,0:T(8,128)} %entries.1, s32[8,1,64,128]{3,2,1,0:T(8,128)} %off_u_in.1, s32[8,1,64,128]{3,2,1,0:T(8,128)} %off_v_in.1, bf16[8,2,8]{2,1,0:T(2,128)(2,1)} %kern.1, s32[8,64]{1,0:T(8,128)} %owner.1), custom_call_target="tpu_custom_call" | custom-call | tf_op jit(solution)/shard_map/correlate_and_grid/pallas_call | solution.py:354
  91.3 1.3 %copy.8 = f32[1,2048]{1,0:T(1,128)} copy(f32[1,2048]{1,0:T(1,128)} %correlate_and_grid.1) | data formatting | bytes 16384

commit v3 on v2

--- a/solution.py
+++ b/solution.py
@@ -25,7 +25,7 @@
 
 
 def chan_kernel(volt, entries, off_u_in, off_v_in, kern, owner, out,
-                xs, neg, gram, got, raw, packed, lists, tab, his, rows, offs_u, offs_v, buf0, buf1, sums,
+                xs, neg, gram, got, raw, packed, lists, tab, his, rows, offs_u, offs_v, found, sums,
                 mine, theirs, dense, send_a, send_b, got_a, got_b, sum_a, sum_b, got_a2, got_b2, sum_z, got_z,
                 raw_sem, v_send, v_recv, l_send, l_recv, own_sem, e_sem, t_send, t_recv,
                 s_a, r_a, s_b, r_b, s_a2, r_a2, s_b2, r_b2, s_z, r_z):
@@ -131,20 +131,19 @@
     lax.fori_loop(0, 8, prepare, 0)
     iota = lambda shape, axis: lax.broadcasted_iota(jnp.int32, shape, axis)
     taps = kern[chip].astype(F32)
-    dist = iota((64, 128), 1) % 32 - iota((64, 128), 0) % 32
-    taps_v = jnp.zeros((64, 128), F32)
+    ro, co = iota((64, 256), 0), iota((64, 256), 1)
+    dist = jnp.where(ro // 32 == co // 128, co % 32 - ro % 32, -1)
+    taps_v = jnp.zeros((64, 256), F32)
     for tap in range(8):
         taps_v = jnp.where(dist == tap, taps[1:2, tap:tap + 1], taps_v)
     taps_v = taps_v.astype(BF16)
-    ro, co = iota((128, 128), 0), iota((128, 128), 1)
-    u = (ro % 8) * 4 + (ro % 64) // 16
-    same = (ro // 64 == co // 64) & ((ro // 8) % 2 == (co // 32) % 2)
-    dist = jnp.where(same, u - co % 32, -1)
-    taps_u = jnp.zeros((128, 128), F32)
+    ro, co = iota((64, 64), 0), iota((64, 64), 1)
+    dist = jnp.where(ro // 32 == co // 32, (ro % 8) * 4 + (ro % 32) // 8 - co % 32, -1)
+    taps_u = jnp.zeros((64, 64), F32)
     for tap in range(8):
         taps_u = jnp.where(dist == tap, taps[0:1, tap:tap + 1], taps_u)
-    taps_u = taps_u.astype(BF16)
-    taps_u = jnp.concatenate([taps_u, taps_u], axis=1)
+    taps_u = jnp.concatenate([taps_u, taps_u], axis=1).astype(BF16)
+    ro = iota((128, 128), 0)
     low = ro % 64
     outer, inner, zq = low // 16, (low // 4) % 4, low % 4
     ys = jnp.where(ro < 64, outer, inner)
@@ -153,8 +152,6 @@
     owners = owner[pl.ds(chip, 1), :]
     owners = jnp.concatenate([owners, owners], axis=1)
     owner_hot = jnp.where(cell == owners, 1.0, 0.0).astype(BF16)
-    ro, co = iota((64, 48), 0), iota((64, 48), 1)
-    spread_ones = jnp.where(jnp.where(co < 32, co // 16, (co - 32) // 8) == ro // 32, 1.0, 0.0).astype(BF16)
 
     for copy in own:
         copy.wait()
@@ -205,60 +202,57 @@
     def line(ref, g, t):
         return jnp.broadcast_to(ref[g, pl.ds(t, 1), :], (16, 128)).astype(jnp.int16)
 
-    def fetch(tp, buf, g):
+    def fetch(tp, g):
         hot = []
         for a in range(2):
             hi = line(his, g, 2 * tp + a)
             hot.append(jnp.concatenate([jnp.where(ids == hi, one, zero) for ids in hot_ids], axis=0))
-        buf[g] = jnp.dot(tab[g], jnp.concatenate(hot, axis=1), preferred_element_type=F32).astype(BF16)
-
-    def place(tp, buf, g, left, right):
+        found[g, tp] = jnp.dot(tab[g], jnp.concatenate(hot, axis=1), preferred_element_type=F32).astype(BF16)
+
+    def fetch_step(tp, carry):
+        for g in range(8):
+            fetch(tp, g)
+        return carry
+
+    lax.fori_loop(0, TILES_CH // 2, fetch_step, 0, unroll=4)
+
+    def place(tp, g, left, right):
         picked = []
         for a in range(2):
             r = line(rows, g, 2 * tp + a)
-            near, mid, far = ids16 == r, hot_ids[1] == r, far_ids == r
             lanes = slice(a * 128, (a + 1) * 128)
-            tiles = [buf[g, n * 16:(n + 1) * 16, lanes] for n in range(5)]
-            re = jnp.where(near, tiles[0], jnp.where(mid, tiles[1], zero))
-            im = jnp.where(near, tiles[2], jnp.where(mid, tiles[3], zero))
-            picked.append(jnp.concatenate([re, im, jnp.where(far, tiles[4], zero)], axis=0))
-        wide = jnp.dot(spread_ones, jnp.concatenate(picked, axis=1), preferred_element_type=F32).astype(BF16)
+            tiles = [found[g, tp, n * 16:(n + 1) * 16, lanes] for n in range(5)]
+            here = [ids == r for ids in hot_ids[:2]]
+            far = jnp.where(far_ids == r, tiles[4], zero).astype(F32)
+            for part in range(2):
+                value = zero
+                for n in range(2):
+                    value = jnp.where(here[n], tiles[part * 2 + n], value)
+                value = value.astype(F32)
+                value = value[:8] + value[8:] + far[part * 8:part * 8 + 8]
+                for step in (4, 2, 1):
+                    value = value + pltpu.roll(value, step, 0)
+                picked.append(jnp.concatenate([value, value], axis=0).astype(BF16))
         for a in range(2):
-            lanes = slice(a * 128, (a + 1) * 128)
             at_u = line(offs_u, g, 2 * tp + a)
             at_v = line(offs_v, g, 2 * tp + a)
-            masks = [ids16 == at_u, hot_ids[1] == at_u]
+            masks = [ids16 == at_v, hot_ids[1] == at_v]
             left[a].append(jnp.concatenate(
-                [jnp.where(masks[n % 2], wide[n * 16:(n + 1) * 16, lanes], zero) for n in range(4)], axis=0))
+                [jnp.where(ids == at_u, one, zero) for ids in (ids16, hot_ids[1])], axis=0))
             right[a].append(jnp.concatenate(
-                [jnp.where(ids == at_v, one, zero) for ids in (ids16, hot_ids[1])], axis=0))
-
-    def stage(tp_next, buf_next, tp, buf):
-        totals = [None, None]
-        for gp in range(4):
-            left, right = [[], []], [[], []]
-            for g in (2 * gp, 2 * gp + 1):
-                fetch(tp_next, buf_next, g)
-                place(tp, buf, g, left, right)
-            for a in range(2):
-                twice = jnp.concatenate(right[a], axis=1)
-                term = dot_nt(jnp.concatenate(left[a], axis=1), jnp.concatenate([twice, twice], axis=0))
-                totals[a] = term if totals[a] is None else totals[a] + term
+                [jnp.where(masks[n % 2], picked[2 * a + n // 2], zero) for n in range(4)], axis=0))
+
+    def place_step(tp, carry):
+        left, right = [[], []], [[], []]
+        for g in range(8):
+            place(tp, g, left, right)
         for a in range(2):
-            sums[2 * tp + a] = totals[a]
-
-    for g in range(8):
-        fetch(0, buf0, g)
-
-    def pair(i, carry):
-        stage(2 * i + 1, buf1, 2 * i, buf0)
-        stage(lax.rem(2 * i + 2, TILES_CH // 2), buf0, 2 * i + 1, buf1)
+            sums[2 * tp + a] = dot_nt(jnp.concatenate(left[a], axis=1), jnp.concatenate(right[a], axis=1))
         return carry
 
-    lax.fori_loop(0, TILES_CH // 4, pair, 0)
-
-    first_lanes = iota((128, 64), 1) < 32
-    lane_grp = iota((16, 128), 1) // 32
+    lax.fori_loop(0, TILES_CH // 2, place_step, 0, unroll=4)
+
+    lane_grp = iota((8, 128), 1) // 32
 
     def tile_copy(step):
         part = pl.ds(pl.multiple_of(step * 8, 8), 8)
@@ -268,18 +262,23 @@
     def finish(step, carry):
         for b in range(4):
             t = step * 8 + b * 2
-            value = sums[pl.ds(t, 2)].reshape(128, 64)
-            high = value.astype(BF16).astype(F32)
-            mixed = jnp.where(first_lanes, high, value - high).astype(BF16)
-            spread = jnp.dot(mixed, taps_v, preferred_element_type=F32)
+            value = sums[pl.ds(t, 2)].reshape(64, 64)
+            high = value.astype(BF16)
+            low_part = (value - high.astype(F32)).astype(BF16)
+            spread = (jnp.dot(high, taps_v, preferred_element_type=F32)
+                      + jnp.dot(low_part, taps_v, preferred_element_type=F32))
             high = spread.astype(BF16)
             low_part = (spread - high.astype(F32)).astype(BF16)
             cells = jnp.dot(taps_u, jnp.concatenate([high, low_part], axis=0), preferred_element_type=F32)
             for a in range(2):
-                tile = cells[a * 64:a * 64 + 16]
-                for ul in range(1, 4):
-                    tile = jnp.where(lane_grp == ul, cells[a * 64 + ul * 16:a * 64 + ul * 16 + 16], tile)
-                mine.reshape(16 * TILES_CH, 128)[pl.ds(t + a, 16, stride=TILES_CH), :] = tile
+                parts = []
+                for part in range(2):
+                    lanes = slice(part * 128, (part + 1) * 128)
+                    tile = cells[a * 32:a * 32 + 8, lanes]
+                    for ul in range(1, 4):
+                        tile = jnp.where(lane_grp == ul, cells[a * 32 + ul * 8:a * 32 + ul * 8 + 8, lanes], tile)
+                    parts.append(tile)
+                mine.reshape(16 * TILES_CH, 128)[pl.ds(t + a, 16, stride=TILES_CH), :] = jnp.concatenate(parts, axis=0)
         tile_copy(step).start()
         return carry
 
@@ -365,8 +364,9 @@
             pltpu.VMEM(lists_shape, jnp.int16),
             pltpu.VMEM(lists_shape, jnp.int16),
             pltpu.VMEM((8, TAB_ROWS, 256), BF16),
-        ] + [pltpu.VMEM((8, TILES_CH, CAP), jnp.int32)] * 4 + [pltpu.VMEM((8, TAB_ROWS, 256), BF16)] * 2 + [
-            pltpu.VMEM((TILES_CH, 64, 64), F32),
+        ] + [pltpu.VMEM((8, TILES_CH, CAP), jnp.int32)] * 4 + [
+            pltpu.VMEM((8, TILES_CH // 2, TAB_ROWS, 256), BF16),
+            pltpu.VMEM((TILES_CH, 32, 64), F32),
             pltpu.VMEM((16, TILES_CH, 128), F32),
             pltpu.VMEM((16, TILES_CH, 128), F32),
             pltpu.VMEM((16, 128, 128), F32),

time: 92.8 us -> 84 us (0.905)
  Pallas kernels: 91.3 us -> 82.5 us
    pallas_call x1, Pallas kernels: 91.3 us -> 82.5 us  [on_device(): pl.pallas_call(chan_kernel, out_shape=jax.ShapeDtypeStruct((1, 2048), F32...]
where the time goes in v3:
time: 84 us; the launch traced here: 83.8 us
  Pallas kernels  82.5 us (98%)
  local copies, waits for them, and re-layouts  1.3 us (2%)
    pallas_call x1, Pallas kernels, on_device(): pl.pallas_call(chan_kernel, out_shape=jax.ShapeDtypeStruct((1, 2048), F32...  82.5 us

profile of v3, /device:TPU:2, one launch (start us, length us, event | category | flops | bytes accessed | tf_op | source)
XLA Modules:
  0.0 83.8 jit_solution(17708054666039881853)
XLA Ops:
  0.0 82.5 %correlate_and_grid.1 = f32[1,2048]{1,0:T(1,128)} custom-call(bf16[8,32,4096]{2,1,0:T(8,128)(2,1)} %volt.1, s32[8,1,64,128]{3,2,1,0:T(8,128)} %entries.1, s32[8,1,64,128]{3,2,1,0:T(8,128)} %off_u_in.1, s32[8,1,64,128]{3,2,1,0:T(8,128)} %off_v_in.1, bf16[8,2,8]{2,1,0:T(2,128)(2,1)} %kern.1, s32[8,64]{1,0:T(8,128)} %owner.1), custom_call_target="tpu_custom_call" | custom-call | tf_op jit(solution)/shard_map/correlate_and_grid/pallas_call | solution.py:353
  82.5 1.3 %copy.8 = f32[1,2048]{1,0:T(1,128)} copy(f32[1,2048]{1,0:T(1,128)} %correlate_and_grid.1) | data formatting | bytes 16384

commit v4 on v3

--- a/solution.py
+++ b/solution.py
@@ -14,7 +14,8 @@
 TILES_CH = 64
 CAP = 128
 GRID_TILES = 256
-TAB_ROWS = 80
+TAB_ROWS = 96
+DEPTH = 192
 N_CHIPS = 8
 F32 = jnp.float32
 BF16 = jnp.bfloat16
@@ -56,23 +57,14 @@
     peers = [(chan, lax.rem(me + j, 16)) for j in range(1, 16)]
     peers += [device(peer_x(d), y, z) for d in (1, 3)]
     peers += [device(x, y, peer_z(d)) for d in range(1, 8)]
-    barrier = pltpu.get_barrier_semaphore()
-    for peer in peers:
-        pl.semaphore_signal(barrier, 1, device_id=peer, device_id_type=MESH)
-
     loads = [pltpu.make_async_copy(ref.at[:, 0], raw.at[n], raw_sem.at[n])
              for n, ref in enumerate((entries, off_u_in, off_v_in))]
     for copy in loads:
         copy.start()
-    for copy in loads:
-        copy.wait()
-
-    def narrow(k, carry):
-        for n in range(3):
-            packed[k, n] = raw[n, k].astype(jnp.int16)
-        return carry
-
-    lax.fori_loop(0, N_CHIPS, narrow, 0)
+    barrier = pltpu.get_barrier_semaphore()
+    for peer in peers:
+        pl.semaphore_signal(barrier, 1, device_id=peer, device_id_type=MESH)
+
     pl.semaphore_wait(barrier, len(peers))
 
     def send(src, dst, ss, rs, peer):
@@ -87,15 +79,6 @@
         return pltpu.make_async_remote_copy(
             packed.at[k], lists.at[list_slot], l_send.at[k], l_recv.at[list_slot],
             device_id=(chan, 2 * k + list_core), device_id_type=MESH)
-
-    for k in range(N_CHIPS):
-        @pl.when(2 * k + list_core != me)
-        def _():
-            list_copy(k).start()
-
-        @pl.when(2 * k + list_core == me)
-        def _():
-            pltpu.make_async_copy(packed.at[k], lists.at[list_slot], l_recv.at[list_slot]).start()
 
     def volt_src(dest, half):
         return volt.at[dest // 2, :, pl.ds(pl.multiple_of(half * 2048 + lax.rem(dest, 2) * 1024, 1024), 1024)]
@@ -113,22 +96,24 @@
     for copy in own:
         copy.start()
 
-    for slot in range(8):
-        pltpu.make_async_copy(packed.at[0], lists.at[slot], l_recv.at[slot]).wait()
-
-    def prepare(g, carry):
-        entry = lists[g, 0].astype(jnp.int32)
-        shift = entry >> 10
-        i = (entry >> 5) & 31
-        j = entry & 31
-        far = shift == 8
-        his[g] = jnp.where(far, (i >> 3) * 32 + j, (shift & 7) * 32 + j)
-        rows[g] = jnp.where(shift > 8, -1, jnp.where(far, 32 + (i & 7), i))
-        offs_u[g] = lists[g, 1].astype(jnp.int32)
-        offs_v[g] = lists[g, 2].astype(jnp.int32)
+    for copy in loads:
+        copy.wait()
+
+    def narrow(k, carry):
+        for n in range(3):
+            packed[k, n] = raw[n, k].astype(jnp.int16)
         return carry
 
-    lax.fori_loop(0, 8, prepare, 0)
+    lax.fori_loop(0, N_CHIPS, narrow, 0)
+    for k in range(N_CHIPS):
+        @pl.when(2 * k + list_core != me)
+        def _():
+            list_copy(k).start()
+
+        @pl.when(2 * k + list_core == me)
+        def _():
+            pltpu.make_async_copy(packed.at[k], lists.at[list_slot], l_recv.at[list_slot]).start()
+
     iota = lambda shape, axis: lax.broadcasted_iota(jnp.int32, shape, axis)
     taps = kern[chip].astype(F32)
     ro, co = iota((64, 256), 0), iota((64, 256), 1)
@@ -173,30 +158,39 @@
     products(core)
     exchange.wait()
 
-    lane, row = iota((GRP, 256), 1), iota((GRP, 256), 0)
-    lane_grp8 = iota((8, 128), 1) // 32
+    lane, row = iota((GRP, 512), 1), iota((GRP, 512), 0)
+    masked = (lane == row) | ((lane >= 256) & (core == 1))
+    low_lanes = iota((16, 256), 1) < 96
     for g in range(8):
-        fars = []
         for part in range(2):
             block = slice(g * GRP, (g + 1) * GRP)
             full = (gram[core, part, block, :] + got[part, block, :]) * (1.0 / 64.0)
             if g:
                 full = pltpu.roll(full, 512 - g * GRP, 1)
-            near = jnp.where(lane == row, 0.0, full[:, :256])
-            tab[g, part * GRP:(part + 1) * GRP, :] = near.astype(BF16)
-            far = jnp.zeros((8, 128), F32)
-            for m in range(4):
-                piece = full[m * 8:(m + 1) * 8, 256:384]
-                if m:
-                    piece = pltpu.roll(piece, m * 32, 1)
-                far = jnp.where(lane_grp8 == m, piece, far)
-            fars.append(jnp.where(core == 0, far, 0.0))
-        far = jnp.concatenate(fars, axis=0)
-        tab[g, 64:80, :] = jnp.concatenate([far, jnp.zeros((16, 128), F32)], axis=1).astype(BF16)
-
+            full = jnp.where(masked, 0.0, full)
+            tab[g, part * GRP:(part + 1) * GRP, :] = full[:, :256].astype(BF16)
+            upper = pltpu.roll(full[:16], 512 - DEPTH, 1)[:, :256]
+            lower = pltpu.roll(full[16:], 512 - DEPTH + 96, 1)[:, :256]
+            tab[g, 64 + part * 16:80 + part * 16, :] = jnp.where(low_lanes, upper, lower).astype(BF16)
+
+    for slot in range(8):
+        pltpu.make_async_copy(packed.at[0], lists.at[slot], l_recv.at[slot]).wait()
+
+    def prepare(g, carry):
+        entry = lists[g, 0].astype(jnp.int32)
+        shift = entry >> 10
+        i = (entry >> 5) & 31
+        j = entry & 31
+        far = shift >= 6
+        his[g] = jnp.where(far, (i >> 4) * 96 + (shift - 6) * 32 + j, shift * 32 + j)
+        rows[g] = jnp.where(shift > 8, -1, jnp.where(far, 32 + (i & 15), i))
+        offs_u[g] = lists[g, 1].astype(jnp.int32)
+        offs_v[g] = lists[g, 2].astype(jnp.int32)
+        return carry
+
+    lax.fori_loop(0, 8, prepare, 0)
     ids16 = iota((16, 128), 0).astype(jnp.int16)
-    hot_ids = [(iota((16, 128), 0) + 16 * n).astype(jnp.int16) for n in range(16)]
-    far_ids = (iota((16, 128), 0) % 8 + 32).astype(jnp.int16)
+    hot_ids = [(iota((16, 128), 0) + 16 * n).astype(jnp.int16) for n in range(DEPTH // 16)]
     one, zero = jnp.ones((), BF16), jnp.zeros((), BF16)
 
     def line(ref, g, t):
@@ -207,29 +201,28 @@
         for a in range(2):
             hi = line(his, g, 2 * tp + a)
             hot.append(jnp.concatenate([jnp.where(ids == hi, one, zero) for ids in hot_ids], axis=0))
-        found[g, tp] = jnp.dot(tab[g], jnp.concatenate(hot, axis=1), preferred_element_type=F32).astype(BF16)
+        found[g, tp] = jnp.dot(tab[g, :, :DEPTH], jnp.concatenate(hot, axis=1), preferred_element_type=F32).astype(BF16)
 
     def fetch_step(tp, carry):
         for g in range(8):
             fetch(tp, g)
         return carry
 
-    lax.fori_loop(0, TILES_CH // 2, fetch_step, 0, unroll=4)
+    lax.fori_loop(0, TILES_CH // 2, fetch_step, 0, unroll=8)
 
     def place(tp, g, left, right):
         picked = []
         for a in range(2):
             r = line(rows, g, 2 * tp + a)
             lanes = slice(a * 128, (a + 1) * 128)
-            tiles = [found[g, tp, n * 16:(n + 1) * 16, lanes] for n in range(5)]
-            here = [ids == r for ids in hot_ids[:2]]
-            far = jnp.where(far_ids == r, tiles[4], zero).astype(F32)
+            tiles = [found[g, tp, n * 16:(n + 1) * 16, lanes] for n in range(6)]
+            here = [ids == r for ids in hot_ids[:3]]
             for part in range(2):
-                value = zero
+                value = jnp.where(here[2], tiles[4 + part], zero)
                 for n in range(2):
                     value = jnp.where(here[n], tiles[part * 2 + n], value)
                 value = value.astype(F32)
-                value = value[:8] + value[8:] + far[part * 8:part * 8 + 8]
+                value = value[:8] + value[8:]
                 for step in (4, 2, 1):
                     value = value + pltpu.roll(value, step, 0)
                 picked.append(jnp.concatenate([value, value], axis=0).astype(BF16))
@@ -242,15 +235,12 @@
             right[a].append(jnp.concatenate(
                 [jnp.where(masks[n % 2], picked[2 * a + n // 2], zero) for n in range(4)], axis=0))
 
-    def place_step(tp, carry):
+    def place_pair(tp):
         left, right = [[], []], [[], []]
         for g in range(8):
             place(tp, g, left, right)
         for a in range(2):
             sums[2 * tp + a] = dot_nt(jnp.concatenate(left[a], axis=1), jnp.concatenate(right[a], axis=1))
-        return carry
-
-    lax.fori_loop(0, TILES_CH // 2, place_step, 0, unroll=4)
 
     lane_grp = iota((8, 128), 1) // 32
 
@@ -259,30 +249,49 @@
         return pltpu.make_async_remote_copy(mine.at[:, part], theirs.at[:, part], t_send.at[step], t_recv.at[step],
                                             device_id=partner, device_id_type=MESH)
 
-    def finish(step, carry):
+    def spread_v(tp):
+        value = sums[pl.ds(2 * tp, 2)].reshape(64, 64)
+        high = value.astype(BF16)
+        low_part = (value - high.astype(F32)).astype(BF16)
+        return (jnp.dot(high, taps_v, preferred_element_type=F32)
+                + jnp.dot(low_part, taps_v, preferred_element_type=F32))
+
+    def spread_u(spread):
+        high = spread.astype(BF16)
+        low_part = (spread - high.astype(F32)).astype(BF16)
+        return jnp.dot(taps_u, jnp.concatenate([high, low_part], axis=0), preferred_element_type=F32)
+
+    def keep(tp, cells):
+        for a in range(2):
+            parts = []
+            for part in range(2):
+                lanes = slice(part * 128, (part + 1) * 128)
+                tile = cells[a * 32:a * 32 + 8, lanes]
+                for ul in range(1, 4):
+                    tile = jnp.where(lane_grp == ul, cells[a * 32 + ul * 8:a * 32 + ul * 8 + 8, lanes], tile)
+                parts.append(tile)
+            mine.reshape(16 * TILES_CH, 128)[pl.ds(2 * tp + a, 16, stride=TILES_CH), :] = jnp.concatenate(parts, axis=0)
+
+    def place_and_finish(step, carry):
+        waiting = None
         for b in range(4):
-            t = step * 8 + b * 2
-            value = sums[pl.ds(t, 2)].reshape(64, 64)
-            high = value.astype(BF16)
-            low_part = (value - high.astype(F32)).astype(BF16)
-            spread = (jnp.dot(high, taps_v, preferred_element_type=F32)
-                      + jnp.dot(low_part, taps_v, preferred_element_type=F32))
-            high = spread.astype(BF16)
-            low_part = (spread - high.astype(F32)).astype(BF16)
-            cells = jnp.dot(taps_u, jnp.concatenate([high, low_part], axis=0), preferred_element_type=F32)
-            for a in range(2):
-                parts = []
-                for part in range(2):
-                    lanes = slice(part * 128, (part + 1) * 128)
-                    tile = cells[a * 32:a * 32 + 8, lanes]
-                    for ul in range(1, 4):
-                        tile = jnp.where(lane_grp == ul, cells[a * 32 + ul * 8:a * 32 + ul * 8 + 8, lanes], tile)
-                    parts.append(tile)
-                mine.reshape(16 * TILES_CH, 128)[pl.ds(t + a, 16, stride=TILES_CH), :] = jnp.concatenate(parts, axis=0)
-        tile_copy(step).start()
+            spread = spread_v(step * 4 - 4 + b)
+            place_pair(step * 4 + b)
+            if waiting is not None:
+                keep(step * 4 - 5 + b, waiting)
+            waiting = spread_u(spread)
+        keep(step * 4 - 1, waiting)
+        tile_copy(step - 1).start()
         return carry
 
-    lax.fori_loop(0, TILES_CH // 8, finish, 0)
+    for b in range(4):
+        place_pair(b)
+    lax.fori_loop(1, TILES_CH // 8, place_and_finish, 0)
+    last = [spread_v(TILES_CH // 2 - 4 + b) for b in range(4)]
+    last = [spread_u(spread) for spread in last]
+    for b in range(4):
+        keep(TILES_CH // 2 - 4 + b, last[b])
+    tile_copy(TILES_CH // 8 - 1).start()
     for step in range(TILES_CH // 8):
         tile_copy(step).wait()
 

time: 84 us -> 73.7 us (0.88)
  Pallas kernels: 82.5 us -> 72.2 us
    pallas_call x1, Pallas kernels: 82.5 us -> 72.2 us  [on_device(): pl.pallas_call(chan_kernel, out_shape=jax.ShapeDtypeStruct((1, 2048), F32...]
where the time goes in v4:
time: 73.7 us; the launch traced here: 73.5 us
  Pallas kernels  72.2 us (98%)
  local copies, waits for them, and re-layouts  1.3 us (2%)
    pallas_call x1, Pallas kernels, on_device(): pl.pallas_call(chan_kernel, out_shape=jax.ShapeDtypeStruct((1, 2048), F32...  72.2 us

profile of v4, /device:TPU:2, one launch (start us, length us, event | category | flops | bytes accessed | tf_op | source)
XLA Modules:
  0.0 73.5 jit_solution(443647735237348633)
XLA Ops:
  0.0 72.2 %correlate_and_grid.1 = f32[1,2048]{1,0:T(1,128)} custom-call(bf16[8,32,4096]{2,1,0:T(8,128)(2,1)} %volt.1, s32[8,1,64,128]{3,2,1,0:T(8,128)} %entries.1, s32[8,1,64,128]{3,2,1,0:T(8,128)} %off_u_in.1, s32[8,1,64,128]{3,2,1,0:T(8,128)} %off_v_in.1, bf16[8,2,8]{2,1,0:T(2,128)(2,1)} %kern.1, s32[8,64]{1,0:T(8,128)} %owner.1), custom_call_target="tpu_custom_call" | custom-call | tf_op jit(solution)/shard_map/correlate_and_grid/pallas_call | solution.py:362
  72.2 1.3 %copy.8 = f32[1,2048]{1,0:T(1,128)} copy(f32[1,2048]{1,0:T(1,128)} %correlate_and_grid.1) | data formatting | bytes 16384

commit v5 on v4

--- a/solution.py
+++ b/solution.py
@@ -25,8 +25,8 @@
     return lax.dot_general(a, b, (((1,), (1,)), ((), ())), preferred_element_type=F32)
 
 
-def chan_kernel(volt, entries, off_u_in, off_v_in, kern, owner, out,
-                xs, neg, gram, got, raw, packed, lists, tab, his, rows, offs_u, offs_v, found, sums,
+def chan_kernel(volt, entries, off_u_in, off_v_in, kern_in, owner_in, out,
+                kern, owner, xs, neg, gram, got, raw, packed, lists, tab, his, rows, offs_u, offs_v, found, sums,
                 mine, theirs, dense, send_a, send_b, got_a, got_b, sum_a, sum_b, got_a2, got_b2, sum_z, got_z,
                 raw_sem, v_send, v_recv, l_send, l_recv, own_sem, e_sem, t_send, t_recv,
                 s_a, r_a, s_b, r_b, s_a2, r_a2, s_b2, r_b2, s_z, r_z):
@@ -54,11 +54,14 @@
         return lax.rem(z + d, 8)
 
     partner = (chan, 2 * chip + 1 - core)
-    peers = [(chan, lax.rem(me + j, 16)) for j in range(1, 16)]
+    peers = [device(x, y, peer_z(d)) for d in (4, 3, 5)]
+    peers += [(chan, lax.rem(me + j, 16)) for j in (12, 13, 11, 10, 14, 4, 5, 3, 8, 9, 7, 6, 2, 15, 1)]
+    peers += [device(x, y, peer_z(d)) for d in (2, 6, 1, 7)]
     peers += [device(peer_x(d), y, z) for d in (1, 3)]
-    peers += [device(x, y, peer_z(d)) for d in range(1, 8)]
     loads = [pltpu.make_async_copy(ref.at[:, 0], raw.at[n], raw_sem.at[n])
              for n, ref in enumerate((entries, off_u_in, off_v_in))]
+    loads.append(pltpu.make_async_copy(kern_in, kern, raw_sem.at[3]))
+    loads.append(pltpu.make_async_copy(owner_in, owner, raw_sem.at[4]))
     for copy in loads:
         copy.start()
     barrier = pltpu.get_barrier_semaphore()
@@ -86,12 +89,14 @@
     def volt_dst(half):
         return xs.at[pl.ds(pl.multiple_of(me * GRP, GRP), GRP), pl.ds(half * 1024, 1024)]
 
+    offsets = [(dx, dy, dc) for dx, dy in ((1, 2), (1, 1), (1, 3), (0, 2), (1, 0), (0, 1), (0, 3), (0, 0))
+               for dc in (0, 1) if dx or dy or dc]
     copies = []
     for half in range(2):
-        for j in range(1, 16):
-            dest = lax.rem(me + j, 16)
-            copies.append(send(volt_src(dest, half), volt_dst(half), v_send.at[half, j - 1],
-                               v_recv.at[half, j - 1], (chan, dest)))
+        for n, (dx, dy, dc) in enumerate(offsets):
+            dest = lax.rem(xhi + dx, 2) * 8 + peer_y(dy) * 2 + lax.rem(core + dc, 2)
+            copies.append(send(volt_src(dest, half), volt_dst(half), v_send.at[half, n],
+                               v_recv.at[half, n], (chan, dest)))
     own = [pltpu.make_async_copy(volt_src(me, half), volt_dst(half), own_sem.at[half]) for half in range(2)]
     for copy in own:
         copy.start()
@@ -295,58 +300,62 @@
     for step in range(TILES_CH // 8):
         tile_copy(step).wait()
 
-    for a in range(16):
-        value = mine[a] + theirs[a]
-        high = value.astype(BF16)
-        low_part = (value - high.astype(F32)).astype(BF16)
-        cells = jnp.dot(owner_hot, jnp.concatenate([high, low_part], axis=0), preferred_element_type=F32)
-        dense[a] = cells
-        for n in range(4):
-            send_a[n, a] = cells[n * 16:(n + 1) * 16].astype(BF16)
-            send_b[n, a] = cells[64 + n * 16:64 + (n + 1) * 16].astype(BF16)
-
-    first = []
-    for d in (2, 1, 3):
-        first.append(send(send_a.at[peer_y(d)], got_a.at[d - 1], s_a.at[d - 1], r_a.at[d - 1],
-                          device(x, peer_y(d), z)))
-        first.append(send(send_b.at[slot_x(peer_x(d))], got_b.at[d - 1], s_b.at[d - 1], r_b.at[d - 1],
-                          device(peer_x(d), y, z)))
-    for copy in first:
-        copy.wait()
     at_a = pl.ds(pl.multiple_of(y * 16, 16), 16)
     at_b = pl.ds(pl.multiple_of(64 + slot_x(x) * 16, 16), 16)
-    for a in range(16):
-        value = dense[a, at_a, :]
-        for d in range(3):
-            value = value + got_a[d, a].astype(F32)
-        sum_a.reshape(256, 128)[pl.ds(a, 16, stride=16), :] = value
-        value = dense[a, at_b, :]
-        for d in range(3):
-            value = value + got_b[d, a].astype(F32)
-        sum_b.reshape(256, 128)[pl.ds(a, 16, stride=16), :] = value
 
     def four(slot):
         return pl.ds(pl.multiple_of(slot * 4, 4), 4)
 
-    second = []
-    for d in (2, 1, 3):
-        second.append(send(sum_a.at[four(slot_x(peer_x(d)))], got_a2.at[d - 1], s_a2.at[d - 1], r_a2.at[d - 1],
-                           device(peer_x(d), y, z)))
-        second.append(send(sum_b.at[four(peer_y(d))], got_b2.at[d - 1], s_b2.at[d - 1], r_b2.at[d - 1],
-                           device(x, peer_y(d), z)))
-    for copy in second:
-        copy.wait()
-    sum_z[0:4] = sum_a[four(slot_x(x))] + got_a2[0] + got_a2[1] + got_a2[2]
-    sum_z[4:8] = sum_b[four(y)] + got_b2[0] + got_b2[1] + got_b2[2]
-    third = []
-    for d in (4, 3, 5, 2, 6, 1, 7):
-        third.append(send(sum_z.at[peer_z(d)], got_z.at[d - 1], s_z.at[d - 1], r_z.at[d - 1],
-                          device(x, y, peer_z(d))))
+    first, second, third = [[], []], [[], []], [[], []]
+    for h in range(2):
+        part = pl.ds(h * 8, 8)
+        for a in range(h * 8, h * 8 + 8):
+            value = mine[a] + theirs[a]
+            high = value.astype(BF16)
+            low_part = (value - high.astype(F32)).astype(BF16)
+            cells = jnp.dot(owner_hot, jnp.concatenate([high, low_part], axis=0), preferred_element_type=F32)
+            dense[a] = cells
+            for n in range(4):
+                send_a[n, a] = cells[n * 16:(n + 1) * 16].astype(BF16)
+                send_b[n, a] = cells[64 + n * 16:64 + (n + 1) * 16].astype(BF16)
+        for d in (2, 1, 3):
+            first[h].append(send(send_a.at[peer_y(d), part], got_a.at[d - 1, part], s_a.at[h, d - 1],
+                                 r_a.at[h, d - 1], device(x, peer_y(d), z)))
+            first[h].append(send(send_b.at[slot_x(peer_x(d)), part], got_b.at[d - 1, part], s_b.at[h, d - 1],
+                                 r_b.at[h, d - 1], device(peer_x(d), y, z)))
+    for h in range(2):
+        part = pl.ds(h * 8, 8)
+        for copy in first[h]:
+            copy.wait()
+        for a in range(h * 8, h * 8 + 8):
+            value = dense[a, at_a, :]
+            for d in range(3):
+                value = value + got_a[d, a].astype(F32)
+            sum_a.reshape(256, 128)[pl.ds(a, 16, stride=16), :] = value
+            value = dense[a, at_b, :]
+            for d in range(3):
+                value = value + got_b[d, a].astype(F32)
+            sum_b.reshape(256, 128)[pl.ds(a, 16, stride=16), :] = value
+        for d in (2, 1, 3):
+            second[h].append(send(sum_a.at[four(slot_x(peer_x(d))), part], got_a2.at[d - 1, :, part],
+                                  s_a2.at[h, d - 1], r_a2.at[h, d - 1], device(peer_x(d), y, z)))
+            second[h].append(send(sum_b.at[four(peer_y(d)), part], got_b2.at[d - 1, :, part],
+                                  s_b2.at[h, d - 1], r_b2.at[h, d - 1], device(x, peer_y(d), z)))
+    for h in range(2):
+        part, rows8 = pl.ds(h * 8, 8), slice(h * 8, h * 8 + 8)
+        for copy in second[h]:
+            copy.wait()
+        sum_z[0:4, rows8] = (sum_a[four(slot_x(x)), rows8] + got_a2[0, :, rows8] + got_a2[1, :, rows8]
+                             + got_a2[2, :, rows8])
+        sum_z[4:8, rows8] = sum_b[four(y), rows8] + got_b2[0, :, rows8] + got_b2[1, :, rows8] + got_b2[2, :, rows8]
+        for d in (4, 3, 5, 2, 6, 1, 7):
+            third[h].append(send(sum_z.at[peer_z(d), part], got_z.at[d - 1, part], s_z.at[h, d - 1],
+                                 r_z.at[h, d - 1], device(x, y, peer_z(d))))
     for k in range(N_CHIPS):
         @pl.when(2 * k + list_core != me)
         def _():
             list_copy(k).wait_send()
-    for copy in third:
+    for copy in third[0] + third[1]:
         copy.wait()
     value = sum_z[z]
     for d in range(7):
@@ -362,9 +371,11 @@
     return pl.pallas_call(
         chan_kernel,
         out_shape=jax.ShapeDtypeStruct((1, 2048), F32),
-        in_specs=[anywhere] * 4 + [vmem] * 2,
+        in_specs=[anywhere] * 6,
         out_specs=vmem,
         scratch_shapes=[
+            pltpu.VMEM(kernels.shape, BF16),
+            pltpu.VMEM(owner_map.shape, jnp.int32),
             pltpu.VMEM((512, 2048), BF16),
             pltpu.VMEM((256, 2048), BF16),
             pltpu.VMEM((2, 2, 256, 512), F32),
@@ -389,10 +400,9 @@
             pltpu.VMEM((3, 4, 16, 128), F32),
             pltpu.VMEM((8, 16, 128), F32),
             pltpu.VMEM((7, 16, 128), F32),
-            dma((3,)), dma((2, 15)), dma((2, 15)), dma((8,)), dma((8,)), dma((2,)), dma((2,)), dma((8,)), dma((8,)),
-            dma((3,)), dma((3,)), dma((3,)), dma((3,)),
-            dma((3,)), dma((3,)), dma((3,)), dma((3,)),
-            dma((7,)), dma((7,)),
+            dma((5,)), dma((2, 15)), dma((2, 15)), dma((8,)), dma((8,)), dma((2,)), dma((2,)), dma((8,)), dma((8,)),
+        ] + [dma((2, 3))] * 8 + [
+            dma((2, 7)), dma((2, 7)),
         ],
         compiler_params=pltpu.CompilerParams(collective_id=0, has_side_effects=True),
         name="correlate_and_grid",

time: 73.7 us -> 70.1 us (0.951); the launches traced: 73.5 us -> 69 us
  Pallas kernels: 72.2 us -> 67.7 us
    pallas_call x1, Pallas kernels: 72.2 us -> 67.7 us  [on_device(): pl.pallas_call(chan_kernel, out_shape=jax.ShapeDtypeStruct((1, 2048), F32...]
where the time goes in v5:
time: 70.1 us; the launch traced here: 69 us
  Pallas kernels  67.7 us (97%)
  local copies, waits for them, and re-layouts  1.3 us (2%)
    pallas_call x1, Pallas kernels, on_device(): pl.pallas_call(chan_kernel, out_shape=jax.ShapeDtypeStruct((1, 2048), F32...  67.7 us

profile of v5, /device:TPU:2, one launch (start us, length us, event | category | flops | bytes accessed | tf_op | source)
XLA Modules:
  0.0 69.0 jit_solution(5071447985372295996)
XLA Ops:
  0.0 67.7 %correlate_and_grid.1 = f32[1,2048]{1,0:T(1,128)} custom-call(bf16[8,32,4096]{2,1,0:T(8,128)(2,1)} %volt.1, s32[8,1,64,128]{3,2,1,0:T(8,128)} %entries.1, s32[8,1,64,128]{3,2,1,0:T(8,128)} %off_u_in.1, s32[8,1,64,128]{3,2,1,0:T(8,128)} %off_v_in.1, bf16[8,2,8]{2,1,0:T(2,128)(2,1)} %kern_in.1, s32[8,64]{1,0:T(8,128)} %owner_in.1), custom_call_target="tpu_custom_call" | custom-call | tf_op jit(solution)/shard_map/correlate_and_grid/pallas_call | solution.py:371
  67.8 1.3 %copy.8 = f32[1,2048]{1,0:T(1,128)} copy(f32[1,2048]{1,0:T(1,128)} %correlate_and_grid.1) | data formatting | bytes 16384
